TPU v7x, 32 devices: a whole 2x2x4 slice. The times are simulated.
32 devices in a mesh: dp: 2 (over x), fsdp: 16 (over z, y, core).
Axes of the slice: x: 2, y: 2, z: 4, core: 2. Of those that a mesh axis runs over, the one named last changes fastest.
Arguments:
- tokens: bfloat16 [32, 256, 1024], P(('dp', 'fsdp')), may hold values from -6 to 6
- segment_ids: int32 [32, 256], P(('dp', 'fsdp')), may hold values from 0 to 3, never falling along the last dimension, each value on 1 to 128 neighbouring positions
- cotangent: bfloat16 [32, 256, 1024], P(('dp', 'fsdp')), may hold values from -6 to 6
- ln_gain: bfloat16 [2, 1024], P(None, ('dp', 'fsdp')), may hold values from 0.5 to 1.5
- ln_bias: bfloat16 [2, 1024], P(None, ('dp', 'fsdp')), may hold values from -1.75 to 1.75
- w_qkv: bfloat16 [2, 1024, 3072], P(None, ('dp', 'fsdp')), may hold values from -0.1875 to 0.1875
- w_out: bfloat16 [2, 1024, 1024], P(None, ('dp', 'fsdp')), may hold values from -0.75 to 0.75
- w_in: bfloat16 [2, 1024, 4096], P(None, ('dp', 'fsdp')), may hold values from -0.1875 to 0.1875
- b_in: bfloat16 [2, 4096], P(None, ('dp', 'fsdp')), may hold values from -3 to 3
- w_fo: bfloat16 [2, 4096, 1024], P(None, ('dp', 'fsdp')), may hold values from -0.125 to 0.125
- b_fo: bfloat16 [2, 1024], P(None, ('dp', 'fsdp')), may hold values from -1.75 to 1.75
Outputs:
- layer_out: bfloat16 [32, 256, 1024], P(('dp', 'fsdp'))
- d_tokens: float32 [32, 256, 1024], P(('dp', 'fsdp'))
- d_ln_gain: float32 [2, 1024], P(None, ('dp', 'fsdp'))
- d_ln_bias: float32 [2, 1024], P(None, ('dp', 'fsdp'))
- d_w_qkv: float32 [2, 1024, 3072], P(None, ('dp', 'fsdp'))
- d_w_out: float32 [2, 1024, 1024], P(None, ('dp', 'fsdp'))
- d_w_in: float32 [2, 1024, 4096], P(None, ('dp', 'fsdp'))
- d_b_in: float32 [2, 4096], P(None, ('dp', 'fsdp'))
- d_w_fo: float32 [2, 4096, 1024], P(None, ('dp', 'fsdp'))
- d_b_fo: float32 [2, 1024], P(None, ('dp', 'fsdp'))
Inputs may be any that keep to these rules, and one draw needn't show every extreme that they name: `segment_ids`: in each row of 256 tokens the protein ids never fall; each of the 4 proteins has 1 to 128 tokens.
All inputs are finite; a program needn't handle non-finite values.
Results may differ from a plain program's by a relative error of at most 0.013.
Values may be sent and summed in bfloat16 or wider, within the bound.
No kernel may reach another device: no remote copies, remote signals or barrier semaphores. Data moves between devices by JAX's collectives and lax.ppermute only.
A program may use at most 320 MiB of HBM per device.

v0:
```python
import jax
import jax.numpy as jnp
from jax import lax
from jax.sharding import PartitionSpec as P

HEADS = 16
HEAD = 64
ROT = 32
LAYERS = 2


layer_eps = 1e-05
gelu_scale = 0.7978845608028654
masked_fill = -1000000000.0


def gelu_tanh(values):
    return (
        0.5 * values * (1.0 + jnp.tanh(gelu_scale * (values + 0.044715 * values * values * values)))
    )


def positions_of(segment_ids):
    last_axis = segment_ids.ndim - 1
    index_grid = lax.broadcasted_iota(jnp.int32, segment_ids.shape, last_axis)
    earlier = jnp.concatenate([segment_ids[..., :1] - 1, segment_ids[..., :-1]], axis=last_axis)
    starts = jnp.where(segment_ids != earlier, index_grid, jnp.zeros_like(index_grid))
    starts = lax.cummax(starts, axis=last_axis)
    return index_grid - starts


def attention_mask(segment_ids):
    length = segment_ids.shape[-1]
    row_index = lax.broadcasted_iota(jnp.int32, (length, length), 0)
    col_index = lax.broadcasted_iota(jnp.int32, (length, length), 1)
    same_doc = segment_ids[:, :, None] == segment_ids[:, None, :]
    return jnp.logical_and(same_doc, (col_index <= row_index)[None])


def rotary_tables(positions, rot_dim):
    half_rot = rot_dim // 2
    frequency = 10000.0 ** (-(jnp.arange(half_rot, dtype=jnp.float32) * 2.0 / rot_dim))
    angles = positions.astype(jnp.float32)[..., None] * frequency
    return (jnp.cos(angles), jnp.sin(angles))


def rotate(values, cosine, sine_table, rot_dim):
    half_rot = rot_dim // 2
    leading = values[..., :half_rot]
    trailing = values[..., half_rot:rot_dim]
    cos_heads = cosine[..., None, :]
    sin_heads = sine_table[..., None, :]
    return jnp.concatenate(
        [
            leading * cos_heads - trailing * sin_heads,
            trailing * cos_heads + leading * sin_heads,
            values[..., rot_dim:],
        ],
        axis=-1,
    )


def unrotate(grads, cosine, sine_table, rot_dim):
    half_rot = rot_dim // 2
    leading = grads[..., :half_rot]
    trailing = grads[..., half_rot:rot_dim]
    cos_heads = cosine[..., None, :]
    sin_heads = sine_table[..., None, :]
    return jnp.concatenate(
        [
            leading * cos_heads + trailing * sin_heads,
            trailing * cos_heads - leading * sin_heads,
            grads[..., rot_dim:],
        ],
        axis=-1,
    )


def layer_norm(hidden, norm_gain, norm_shift):
    mean_value = jnp.mean(hidden, axis=-1, keepdims=True)
    centered = hidden - mean_value
    variance = jnp.mean(centered * centered, axis=-1, keepdims=True)
    return centered * lax.rsqrt(variance + layer_eps) * norm_gain + norm_shift


def gather_layer(norm_gain, norm_shift, wq_part, wo_part, wi_part, bi_part, wf_part, bf_part):
    return (
        lax.all_gather(norm_gain, ("dp", "fsdp"), axis=0, tiled=True),
        lax.all_gather(norm_shift, ("dp", "fsdp"), axis=0, tiled=True),
        lax.all_gather(wq_part, ("dp", "fsdp"), axis=0, tiled=True),
        lax.all_gather(wo_part, ("dp", "fsdp"), axis=0, tiled=True),
        lax.all_gather(wi_part, ("dp", "fsdp"), axis=0, tiled=True),
        lax.all_gather(bi_part, ("dp", "fsdp"), axis=0, tiled=True),
        lax.all_gather(wf_part, ("dp", "fsdp"), axis=0, tiled=True),
        lax.all_gather(bf_part, ("dp", "fsdp"), axis=0, tiled=True),
    )


def flatten_rows(matrix):
    return matrix.reshape(-1, 128)


def scatter_layer(grads):
    widths = [item.shape[1] if item.ndim == 2 else 0 for item in grads]
    flat = [flatten_rows(item) if item.ndim == 2 else item for item in grads]
    summed = (
        lax.psum_scatter(flat[0], ("dp", "fsdp"), scatter_dimension=0, tiled=True),
        lax.psum_scatter(flat[1], ("dp", "fsdp"), scatter_dimension=0, tiled=True),
        lax.psum_scatter(flat[2], ("dp", "fsdp"), scatter_dimension=0, tiled=True),
        lax.psum_scatter(flat[3], ("dp", "fsdp"), scatter_dimension=0, tiled=True),
        lax.psum_scatter(flat[4], ("dp", "fsdp"), scatter_dimension=0, tiled=True),
        lax.psum_scatter(flat[5], ("dp", "fsdp"), scatter_dimension=0, tiled=True),
        lax.psum_scatter(flat[6], ("dp", "fsdp"), scatter_dimension=0, tiled=True),
        lax.psum_scatter(flat[7], ("dp", "fsdp"), scatter_dimension=0, tiled=True),
    )
    return [
        summed[member].reshape(-1, widths[member]) if widths[member] > 0 else summed[member]
        for member in range(8)
    ]


def attention_scores(rot_query, rot_key, allowed):
    scores = jnp.einsum(
        "gshe,gthe->ghst", rot_query, rot_key, preferred_element_type=jnp.float32
    ) * HEAD ** (-0.5)
    return jnp.where(allowed, scores, masked_fill)


def layer_forward(hidden, full_weights, allowed, cosine, sine_table):
    norm_gain, norm_shift, wq_all, wo_all, wi_all, bi_all, wf_all, bf_all = full_weights
    seq_count = allowed.shape[0]
    seq_len = allowed.shape[2]
    model_width = hidden.shape[1]
    heads_shape = (seq_count, seq_len, HEADS, HEAD)
    normed = layer_norm(
        hidden, norm_gain.astype(jnp.float32), norm_shift.astype(jnp.float32)
    ).astype(jnp.bfloat16)
    projected = jnp.dot(normed, wq_all, preferred_element_type=jnp.float32)
    query_rows = projected[:, :model_width].reshape(heads_shape)
    key_rows = projected[:, model_width : 2 * model_width].reshape(heads_shape)
    value_low = projected[:, 2 * model_width :].reshape(heads_shape).astype(jnp.bfloat16)
    rot_query = rotate(query_rows, cosine, sine_table, ROT).astype(jnp.bfloat16)
    rot_key = rotate(key_rows, cosine, sine_table, ROT).astype(jnp.bfloat16)
    scores = attention_scores(rot_query, rot_key, allowed)
    row_max = jnp.max(scores, axis=-1, keepdims=True)
    exponent = jnp.exp(scores - row_max)
    row_total = jnp.sum(exponent, axis=-1, keepdims=True)
    weights_attn = (exponent / row_total).astype(jnp.bfloat16)
    attended = jnp.einsum(
        "ghst,gthe->gshe", weights_attn, value_low, preferred_element_type=jnp.float32
    )
    attended = attended.reshape(seq_count * seq_len, model_width).astype(jnp.bfloat16)
    branch = jnp.dot(attended, wo_all, preferred_element_type=jnp.float32)
    pre_act = jnp.dot(normed, wi_all, preferred_element_type=jnp.float32) + bi_all.astype(
        jnp.float32
    )
    activation = gelu_tanh(pre_act).astype(jnp.bfloat16)
    mlp_out = jnp.dot(activation, wf_all, preferred_element_type=jnp.float32) + bf_all.astype(
        jnp.float32
    )
    kept = (
        hidden,
        normed,
        rot_query,
        rot_key,
        value_low,
        row_max,
        row_total,
        attended,
        pre_act,
        activation,
    )
    return (kept, hidden + branch + mlp_out)


def layer_backward(grad, full_weights, kept, allowed, cosine, sine_table):
    norm_gain, norm_shift, wq_all, wo_all, wi_all, bi_all, wf_all, bf_all = full_weights
    (
        hidden,
        normed,
        rot_query,
        rot_key,
        value_low,
        row_max,
        row_total,
        attended,
        pre_act,
        activation,
    ) = kept
    seq_count = allowed.shape[0]
    seq_len = allowed.shape[2]
    model_width = hidden.shape[1]
    heads_shape = (seq_count, seq_len, HEADS, HEAD)
    grad_low = grad.astype(jnp.bfloat16)
    d_bias_out = jnp.sum(grad_low, axis=0, dtype=jnp.float32)
    d_weight_out = jnp.dot(activation.T, grad_low, preferred_element_type=jnp.float32)
    d_act = jnp.dot(grad_low, wf_all.T, preferred_element_type=jnp.float32)
    unused, gelu_pull = jax.vjp(gelu_tanh, pre_act)
    d_pre = gelu_pull(d_act)[0].astype(jnp.bfloat16)
    d_bias_in = jnp.sum(d_pre, axis=0, dtype=jnp.float32)
    d_weight_in = jnp.dot(normed.T, d_pre, preferred_element_type=jnp.float32)
    d_proj_out = jnp.dot(attended.T, grad_low, preferred_element_type=jnp.float32)
    d_attended = (
        jnp.dot(grad_low, wo_all.T, preferred_element_type=jnp.float32)
        .astype(jnp.bfloat16)
        .reshape(heads_shape)
    )
    scores = attention_scores(rot_query, rot_key, allowed)
    probs_full = jnp.exp(scores - row_max) / row_total
    probs_low = probs_full.astype(jnp.bfloat16)
    d_values = jnp.einsum(
        "ghst,gshe->gthe", probs_low, d_attended, preferred_element_type=jnp.float32
    )
    d_probs = jnp.einsum(
        "gshe,gthe->ghst", d_attended, value_low, preferred_element_type=jnp.float32
    )
    row_dot = jnp.sum(probs_full * d_probs, axis=-1, keepdims=True)
    d_scores = (probs_full * (d_probs - row_dot)).astype(jnp.bfloat16)
    d_rot_query = jnp.einsum(
        "ghst,gthe->gshe", d_scores, rot_key, preferred_element_type=jnp.float32
    ) * HEAD ** (-0.5)
    d_rot_key = jnp.einsum(
        "ghst,gshe->gthe", d_scores, rot_query, preferred_element_type=jnp.float32
    ) * HEAD ** (-0.5)
    d_query = unrotate(d_rot_query, cosine, sine_table, ROT)
    d_key = unrotate(d_rot_key, cosine, sine_table, ROT)
    row_count = seq_count * seq_len
    d_qkv = jnp.concatenate(
        [
            d_query.reshape(row_count, model_width),
            d_key.reshape(row_count, model_width),
            d_values.reshape(row_count, model_width),
        ],
        axis=1,
    ).astype(jnp.bfloat16)
    d_weight_qkv = jnp.dot(normed.T, d_qkv, preferred_element_type=jnp.float32)
    d_normed = jnp.dot(d_qkv, wq_all.T, preferred_element_type=jnp.float32) + jnp.dot(
        d_pre, wi_all.T, preferred_element_type=jnp.float32
    )
    unused_norm, norm_pull = jax.vjp(
        layer_norm, hidden, norm_gain.astype(jnp.float32), norm_shift.astype(jnp.float32)
    )
    d_hidden, d_gain, d_shift = norm_pull(d_normed)
    grads = (
        d_gain,
        d_shift,
        d_weight_qkv,
        d_proj_out,
        d_weight_in,
        d_bias_in,
        d_weight_out,
        d_bias_out,
    )
    return (grad + d_hidden, grads)


def on_device(
    tokens, segment_ids, cotangent, ln_gain, ln_bias, w_qkv, w_out, w_in, b_in, w_fo, b_fo
):
    seq_count, seq_len, model_width = tokens.shape
    row_count = seq_count * seq_len
    positions = positions_of(segment_ids)
    cosine, sine_table = rotary_tables(positions, ROT)
    allowed = attention_mask(segment_ids)[:, None]
    hidden = tokens.astype(jnp.float32).reshape(row_count, model_width)
    saved = []
    for depth in range(LAYERS):
        full_weights = gather_layer(
            ln_gain[depth],
            ln_bias[depth],
            w_qkv[depth],
            w_out[depth],
            w_in[depth],
            b_in[depth],
            w_fo[depth],
            b_fo[depth],
        )
        kept, hidden = layer_forward(hidden, full_weights, allowed, cosine, sine_table)
        saved.append((None, kept))
    layer_out = hidden.astype(jnp.bfloat16).reshape(seq_count, seq_len, model_width)
    grad = cotangent.astype(jnp.float32).reshape(row_count, model_width)
    owned = []
    for depth in range(LAYERS - 1, -1, -1):
        full_weights = (
            lax.all_gather(ln_gain[depth], ("dp", "fsdp"), axis=0, tiled=True),
            lax.all_gather(ln_bias[depth], ("dp", "fsdp"), axis=0, tiled=True),
            lax.all_gather(w_qkv[depth], ("dp", "fsdp"), axis=0, tiled=True),
            lax.all_gather(w_out[depth], ("dp", "fsdp"), axis=0, tiled=True),
            lax.all_gather(w_in[depth], ("dp", "fsdp"), axis=0, tiled=True),
            lax.all_gather(b_in[depth], ("dp", "fsdp"), axis=0, tiled=True),
            lax.all_gather(w_fo[depth], ("dp", "fsdp"), axis=0, tiled=True),
            lax.all_gather(b_fo[depth], ("dp", "fsdp"), axis=0, tiled=True),
        )
        grad, grads = layer_backward(
            grad, full_weights, saved[depth][1], allowed, cosine, sine_table
        )
        owned.append(scatter_layer(grads))
    owned = owned[::-1]
    stacked = [
        jnp.stack([owned[depth][member] for depth in range(LAYERS)], axis=0) for member in range(8)
    ]
    d_tokens = grad.reshape(seq_count, seq_len, model_width)
    return (
        layer_out,
        d_tokens,
        stacked[0],
        stacked[1],
        stacked[2],
        stacked[3],
        stacked[4],
        stacked[5],
        stacked[6],
        stacked[7],
    )


def solution(mesh):
    placed = (
        P(("dp", "fsdp"), None, None),
        P(("dp", "fsdp"), None),
        P(("dp", "fsdp"), None, None),
        P(None, ("dp", "fsdp")),
        P(None, ("dp", "fsdp")),
        P(None, ("dp", "fsdp"), None),
        P(None, ("dp", "fsdp"), None),
        P(None, ("dp", "fsdp"), None),
        P(None, ("dp", "fsdp")),
        P(None, ("dp", "fsdp"), None),
        P(None, ("dp", "fsdp")),
    )
    return jax.shard_map(
        on_device,
        mesh=mesh,
        in_specs=placed,
        out_specs=(
            P(("dp", "fsdp"), None, None),
            P(("dp", "fsdp"), None, None),
            P(None, ("dp", "fsdp")),
            P(None, ("dp", "fsdp")),
            P(None, ("dp", "fsdp"), None),
            P(None, ("dp", "fsdp"), None),
            P(None, ("dp", "fsdp"), None),
            P(None, ("dp", "fsdp")),
            P(None, ("dp", "fsdp"), None),
            P(None, ("dp", "fsdp")),
        ),
        check_vma=False,
    )
```

profile of v0, /device:TPU:19, one launch (start us, length us, event | category | flops | bytes accessed | tf_op | source)
XLA Modules:
  0.0 1971.8 jit_solution(2211329896247742117)
XLA Ops:
  20.7 40.0 %all-reduce.15 = (bf16[1024]{0:T(1024)(128)(2,1)}, bf16[1024]{0:T(1024)(128)(2,1)S(1)}, bf16[1024]{0:T(1024)(128)(2,1)S(1)}, bf16[1024]{0:T(1024)(128)(2,1)S(1)}...) all-reduce(bf16[1024]{0:T(1024)(128)(2,1)S(1)} %dynamic-update-slic, ...), channel_id=17, replica_groups=mesh['dp'=2,'fsdp'=16] {'dp','fsdp'}, use_global_device_ids=true, to_apply=%add.5 | all-reduce | flops 6144 | bytes 24576
  62.5 34.1 %all-gather.13 = bf16[1,4096]{1,0:T(2,128)(2,1)S(1)} all-gather(bf16[1,128]{1,0:T(2,128)(2,1)S(1)} %get-tuple-element.75), channel_id=15, replica_groups=mesh['dp'=2,'fsdp'=16] {'dp','fsdp'}, dimensions={1}, use_global_device_ids=true | all-gather | bytes 8448 | tf_op jit(solution)/shard_map/all_gather | solution.py:93
  97.2 36.9 %all-gather.5 = bf16[1,4096]{1,0:T(2,128)(2,1)S(1)} all-gather(bf16[1,128]{1,0:T(2,128)(2,1)S(1)} %get-tuple-element.76), channel_id=7, replica_groups=mesh['dp'=2,'fsdp'=16] {'dp','fsdp'}, dimensions={1}, use_global_device_ids=true | all-gather | bytes 8448 | tf_op jit(solution)/shard_map/all_gather | solution.py:93
  141.4 4.7 fusion.24
  153.3 4.5 fusion.175
  160.6 60.4 %all-gather.29.cloned.1.call-done = bf16[1,1024,4096]{2,1,0:T(8,128)(2,1)} async-done(((bf16[1,32,4096]{2,1,0:T(8,128)(2,1)}), bf16[1,1024,4096]{2,1,0:T(8,128)(2,1)}) %all-gather.29.cloned.1.call-update) | async-done | bytes 8388624 | tf_op jit(solution)/shard_map/all_gather | solution.py:92
  221.0 7.8 fusion.26
  228.8 71.7 %all-gather.31.cloned.1.call-done = bf16[1,4096,1024]{2,1,0:T(8,128)(2,1)} async-done(((bf16[1,128,1024]{2,1,0:T(8,128)(2,1)}), bf16[1,4096,1024]{2,1,0:T(8,128)(2,1)}) %all-gather.31.cloned.1.call-update) | async-done | bytes 8388624 | tf_op jit(solution)/shard_map/all_gather | solution.py:94
  300.5 8.4 fusion.91
  308.9 48.3 %all-gather.27.cloned.1.call-done = bf16[1,1024,1024]{2,1,0:T(8,128)(2,1)} async-done(((bf16[1,32,1024]{2,1,0:T(8,128)(2,1)}), bf16[1,1024,1024]{2,1,0:T(8,128)(2,1)}) %all-gather.27.cloned.1.call-update) | async-done | bytes 2097168 | tf_op jit(solution)/shard_map/all_gather | solution.py:91
  360.4 69.5 %all-gather.33.cloned.1.call-done = bf16[1,1024,3072]{2,1,0:T(8,128)(2,1)} async-done(((bf16[1,32,3072]{2,1,0:T(8,128)(2,1)}), bf16[1,1024,3072]{2,1,0:T(8,128)(2,1)}) %all-gather.33.cloned.1.call-update) | async-done | bytes 6291472 | tf_op jit(solution)/shard_map/all_gather | solution.py:90
  429.9 4.8 fusion.20
  449.3 5.4 fusion.177
  454.6 3.5 multiply_reduce_fusion.1
  464.7 44.3 %all-gather.37.cloned.1.call-done = bf16[1,1024,4096]{2,1,0:T(8,128)(2,1)} async-done(((bf16[1,32,4096]{2,1,0:T(8,128)(2,1)}), bf16[1,1024,4096]{2,1,0:T(8,128)(2,1)}) %all-gather.37.cloned.1.call-update) | async-done | bytes 8388624 | tf_op jit(solution)/shard_map/all_gather | solution.py:92
  509.0 7.8 fusion.29
  516.8 71.3 %all-gather.39.cloned.1.call-done = bf16[1,4096,1024]{2,1,0:T(8,128)(2,1)} async-done(((bf16[1,128,1024]{2,1,0:T(8,128)(2,1)}), bf16[1,4096,1024]{2,1,0:T(8,128)(2,1)}) %all-gather.39.cloned.1.call-update) | async-done | bytes 8388624 | tf_op jit(solution)/shard_map/all_gather | solution.py:94
  588.1 9.8 convert_reduce_fusion
  600.4 5.5 multiply_reduce_fusion.2
  610.8 4.9 reshape.584
  619.4 2.8 fusion.125
  622.2 4.9 reshape.585
  627.4 3.1 fusion.100
  631.8 3.2 multiply_reduce_fusion
  639.6 6.6 fusion.121
  646.2 14.0 reshape.582
  661.4 7.5 fusion.122
  668.9 13.8 reshape.583
  682.8 10.8 fusion.159
  693.6 18.0 reshape.588
  711.9 10.8 fusion.123
  722.7 18.0 reshape.589
  740.8 9.7 fusion.179
  750.5 18.0 reshape.587
  768.6 8.6 convert_reduce_fusion.1
  778.6 8.4 fusion.160
  787.0 18.0 reshape.586
  805.7 6.5 fusion.14
  812.3 4.9 fusion.165
  819.4 39.6 %all-reduce.14 = (f32[1024]{0:T(1024)S(1)}, f32[1024]{0:T(1024)S(1)}, f32[1024]{0:T(1024)S(1)}, f32[1024]{0:T(1024)S(1)}, f32[4096]{0:T(1024)S(1)}, /*index=5*/f...) all-reduce(f32[1024]{0:T(1024)S(1)} %copy-done.71, ...), channel_id=19, replica_groups=mesh['dp'=2,'fsdp'=16] {'dp','fsdp'}, use_global_device_ids=true, to_apply=%region_19.20.clone | all-reduce | flops 14336 | bytes 114688
  861.9 7.5 fusion.94
  871.9 6.2 reduce-scatter.15.cloned.1.call-done
  879.8 171.4 %reduce-scatter.9.cloned.1.call-done = f32[768,128]{1,0:T(8,128)} async-done(((f32[24576,128]{1,0:T(8,128)}), f32[768,128]{1,0:T(8,128)}) %reduce-scatter.9.cloned.1.call-update) | async-done | bytes 393232 | tf_op jit(solution)/shard_map/reduce_scatter | solution.py:109
  1052.3 160.3 %reduce-scatter.11.cloned.1.call-done = f32[768,128]{1,0:T(8,128)} async-done(((f32[24576,128]{1,0:T(8,128)}), f32[768,128]{1,0:T(8,128)}) %reduce-scatter.11.cloned.1.call-update) | async-done | bytes 393232 | tf_op jit(solution)/shard_map/reduce_scatter | solution.py:109
  1214.6 186.2 %reduce-scatter.21.cloned.1.call-done = f32[1024,128]{1,0:T(8,128)} async-done(((f32[32768,128]{1,0:T(8,128)}), f32[1024,128]{1,0:T(8,128)}) %reduce-scatter.21.cloned.1.call-update) | async-done | bytes 524304 | tf_op jit(solution)/shard_map/reduce_scatter | solution.py:113
  1401.9 186.7 %reduce-scatter.23.cloned.1.call-done = f32[1024,128]{1,0:T(8,128)} async-done(((f32[32768,128]{1,0:T(8,128)}), f32[1024,128]{1,0:T(8,128)}) %reduce-scatter.23.cloned.1.call-update) | async-done | bytes 524304 | tf_op jit(solution)/shard_map/reduce_scatter | solution.py:113
  1589.7 185.8 %reduce-scatter.19.cloned.1.call-done = f32[1024,128]{1,0:T(8,128)} async-done(((f32[32768,128]{1,0:T(8,128)}), f32[1024,128]{1,0:T(8,128)}) %reduce-scatter.19.cloned.1.call-update) | async-done | bytes 524304 | tf_op jit(solution)/shard_map/reduce_scatter | solution.py:111
  1777.7 185.0 %reduce-scatter.17.cloned.1.call-done = f32[1024,128]{1,0:T(8,128)} async-done(((f32[32768,128]{1,0:T(8,128)}), f32[1024,128]{1,0:T(8,128)}) %reduce-scatter.17.cloned.1.call-update) | async-done | bytes 524304 | tf_op jit(solution)/shard_map/reduce_scatter | solution.py:111
  (316 shorter events, 95.7 us)
Async XLA Ops:
  7.2 10.2 copy-start.58
  7.2 12.1 copy-start.75
  7.2 12.3 copy-start.76
  7.2 12.8 copy-start.77
  7.2 55.2 %copy-start.78 = (bf16[2,128]{1,0:T(2,128)(2,1)S(1)}, bf16[2,128]{1,0:T(2,128)(2,1)}, u32[]{:S(2)}) copy-start(bf16[2,128]{1,0:T(2,128)(2,1)} %param.19) | copy-start | bytes 1540
  7.2 127.5 %copy-start = (bf16[1,256,1024]{2,1,0:T(8,128)(2,1)S(1)}, bf16[1,256,1024]{2,1,0:T(8,128)(2,1)}, u32[]{:S(2)}) copy-start(bf16[1,256,1024]{2,1,0:T(8,128)(2,1)} %param.11) | copy-start | bytes 1572868
  7.2 129.5 %copy-start.5 = (bf16[1,256,1024]{2,1,0:T(8,128)(2,1)S(1)}, bf16[1,256,1024]{2,1,0:T(8,128)(2,1)}, u32[]{:S(2)}) copy-start(bf16[1,256,1024]{2,1,0:T(8,128)(2,1)} %param.13) | copy-start | bytes 1572868
  7.2 129.5 %all-gather.35.cloned.1.call-start = ((), (), s32[]{:S(2)}) async-start(), calls=%async_computation.21 | async-start | bytes 2162688 | tf_op jit(solution)/shard_map/all_gather | solution.py:91
  8.9 132.4 %all-gather.25.cloned.1.call-start = ((), (), s32[]{:S(2)}) async-start(), calls=%async_computation.16 | async-start | bytes 6488064 | tf_op jit(solution)/shard_map/all_gather | solution.py:90
  10.8 210.2 %all-gather.29.cloned.1.call-start = ((), (), s32[]{:S(2)}) async-start(), calls=%async_computation.18 | async-start | bytes 8650752 | tf_op jit(solution)/shard_map/all_gather | solution.py:92
  12.7 287.8 %all-gather.31.cloned.1.call-start = ((), (), s32[]{:S(2)}) async-start(), calls=%async_computation.19 | async-start | bytes 8650752 | tf_op jit(solution)/shard_map/all_gather | solution.py:94
  14.6 342.5 %all-gather.27.cloned.1.call-start = ((), (), s32[]{:S(2)}) async-start(), calls=%async_computation.17 | async-start | bytes 2162688 | tf_op jit(solution)/shard_map/all_gather | solution.py:91
  15.2 414.7 %all-gather.33.cloned.1.call-start = ((), (), s32[]{:S(2)}) async-start(), calls=%async_computation.20 | async-start | bytes 6488064 | tf_op jit(solution)/shard_map/all_gather | solution.py:90
  15.8 493.2 %all-gather.37.cloned.1.call-start = ((), (), s32[]{:S(2)}) async-start(), calls=%async_computation.22 | async-start | bytes 8650752 | tf_op jit(solution)/shard_map/all_gather | solution.py:92
  16.6 571.5 %all-gather.39.cloned.1.call-start = ((), (), s32[]{:S(2)}) async-start(), calls=%async_computation.23 | async-start | bytes 8650752 | tf_op jit(solution)/shard_map/all_gather | solution.py:94
  17.3 853.7 %reduce-scatter.13.cloned.1.call-start = ((), (), s32[]{:S(2)}) async-start(), calls=%async_computation.10 | async-start | bytes 4325376 | tf_op jit(solution)/shard_map/reduce_scatter | solution.py:110
  135.1 10.9 copy-start.65
  152.0 5.8 copy-start.29
  152.0 5.8 copy-start.31
  152.0 5.8 copy-start.33
  157.8 63.1 %copy-start.60 = (f32[1,4096]{1,0:T(1,128)S(1)}, f32[1,4096]{1,0:T(1,128)}, u32[]{:S(2)}) copy-start(f32[1,4096]{1,0:T(1,128)} %convert_element_type.203) | copy-start | bytes 49156
  221.0 79.5 %copy-start.73 = (f32[1024]{0:T(1024)S(1)}, f32[1024]{0:T(1024)}, u32[]{:S(2)}) copy-start(f32[1024]{0:T(1024)} %convert_element_type.211) | copy-start | bytes 12292
  308.9 51.3 %copy-start.49 = (f32[1024]{0:T(1024)S(1)}, f32[1024]{0:T(1024)}, u32[]{:S(2)}) copy-start(f32[1024]{0:T(1024)} %convert_element_type.212) | copy-start | bytes 12292
  308.9 51.3 %copy-start.56 = (f32[1024]{0:T(1024)S(1)}, f32[1024]{0:T(1024)}, u32[]{:S(2)}) copy-start(f32[1024]{0:T(1024)} %convert_element_type.213) | copy-start | bytes 12292
  359.8 246.0 %copy-start.1 = (f32[256,1024]{1,0:T(8,128)}, f32[256,1024]{1,0:T(8,128)S(1)}, u32[]{:S(2)}) copy-start(f32[256,1024]{1,0:T(8,128)S(1)} %get-tuple-element.86) | copy-start | bytes 3145732
  359.9 74.9 %copy-start.61 = (f32[256]{0:T(256)}, f32[256]{0:T(256)S(1)}, u32[]{:S(2)}) copy-start(f32[256]{0:T(256)S(1)} %broadcast_multiply_fusion) | copy-start | bytes 3076
  360.1 74.6 %copy-start.67 = (f32[256]{0:T(256)}, f32[256]{0:T(256)S(1)}, u32[]{:S(2)}) copy-start(f32[256]{0:T(256)S(1)} %multiply_reduce_fusion.4) | copy-start | bytes 3076
  360.2 74.6 %copy-start.63 = (f32[256]{0:T(256)}, f32[256]{0:T(256)S(1)}, u32[]{:S(2)}) copy-start(f32[256]{0:T(256)S(1)} %fusion.149) | copy-start | bytes 3076
  463.2 45.9 %copy-start.59 = (f32[1,4096]{1,0:T(1,128)S(1)}, f32[1,4096]{1,0:T(1,128)}, u32[]{:S(2)}) copy-start(f32[1,4096]{1,0:T(1,128)} %convert_element_type.207) | copy-start | bytes 49156
  588.1 9.8 copy-start.79
  600.4 5.5 copy-start.68
  615.7 262.4 %reduce-scatter.15.cloned.1.call-start = ((), (), s32[]{:S(2)}) async-start(), calls=%async_computation.11 | async-start | bytes 4325376 | tf_op jit(solution)/shard_map/reduce_scatter | solution.py:110
  627.2 424.0 %reduce-scatter.9.cloned.1.call-start = ((), (), s32[]{:S(2)}) async-start(), calls=%async_computation.8 | async-start | bytes 12976128 | tf_op jit(solution)/shard_map/reduce_scatter | solution.py:109
  639.4 6.8 copy-start.27
  660.2 552.4 %reduce-scatter.11.cloned.1.call-start = ((), (), s32[]{:S(2)}) async-start(), calls=%async_computation.9 | async-start | bytes 12976128 | tf_op jit(solution)/shard_map/reduce_scatter | solution.py:109
  682.7 718.0 %reduce-scatter.21.cloned.1.call-start = ((), (), s32[]{:S(2)}) async-start(), calls=%async_computation.14 | async-start | bytes 17301504 | tf_op jit(solution)/shard_map/reduce_scatter | solution.py:113
  711.6 877.0 %reduce-scatter.23.cloned.1.call-start = ((), (), s32[]{:S(2)}) async-start(), calls=%async_computation.15 | async-start | bytes 17301504 | tf_op jit(solution)/shard_map/reduce_scatter | solution.py:113
  740.7 1034.8 %reduce-scatter.19.cloned.1.call-start = ((), (), s32[]{:S(2)}) async-start(), calls=%async_computation.13 | async-start | bytes 17301504 | tf_op jit(solution)/shard_map/reduce_scatter | solution.py:111
  768.5 1194.1 %reduce-scatter.17.cloned.1.call-start = ((), (), s32[]{:S(2)}) async-start(), calls=%async_computation.12 | async-start | bytes 17301504 | tf_op jit(solution)/shard_map/reduce_scatter | solution.py:111
  805.7 6.6 copy-start.15
  805.7 6.6 copy-start.17
  805.7 6.6 copy-start.28
  812.3 5.0 copy-start.66
  812.3 5.5 copy-start.4
  812.3 5.5 copy-start.70
  861.9 7.5 copy-start.2
  861.9 7.5 copy-start.9
  861.9 7.5 copy-start.18
  (48 other events, 104.0 us)
Sparse Core Ops, SparseCore 0:
  11.5 56.6 all-gather.34
  71.7 69.6 all-gather.24
  144.8 76.1 all-gather.28
  224.3 76.1 all-gather.30
  303.2 53.9 all-gather.26
  360.5 69.3 all-gather.32
  432.8 76.1 all-gather.36
  511.9 76.1 all-gather.38
  615.8 122.5 reduce-scatter.12
  740.6 137.4 reduce-scatter.14
  884.1 167.0 reduce-scatter.8
  1058.1 154.4 reduce-scatter.10
  1214.9 185.8 reduce-scatter.20
  1402.9 185.6 reduce-scatter.22
  1590.7 184.6 reduce-scatter.18
  1777.6 184.9 reduce-scatter.16
where the time goes:
time: 1980 us; the launch traced here: 1970 us
  waiting for transfers between devices  1450 us (73%)
  matrix products  175 us (9%)
  local copies, waits for them, and re-layouts  156 us (8%)
  blocking collectives  151 us (8%)
  other arithmetic  22.6 us (1%)
    reduce_scatter x2, waiting for transfers between devices, scatter_layer(): lax.psum_scatter(flat[6], ('dp', 'fsdp'), scatter_dimension=0, tiled=True)  373 us
    reduce_scatter x2, waiting for transfers between devices, scatter_layer(): lax.psum_scatter(flat[4], ('dp', 'fsdp'), scatter_dimension=0, tiled=True)  371 us
    reduce_scatter x2, waiting for transfers between devices, scatter_layer(): lax.psum_scatter(flat[2], ('dp', 'fsdp'), scatter_dimension=0, tiled=True)  332 us
    all_gather x2, waiting for transfers between devices, gather_layer(): lax.all_gather(wf_part, ('dp', 'fsdp'), axis=0, tiled=True)  143 us
    reshape x8, local copies, waits for them, and re-layouts, flatten_rows(): return matrix.reshape(-1, 128)  110 us
    all_gather x2, waiting for transfers between devices, gather_layer(): lax.all_gather(wi_part, ('dp', 'fsdp'), axis=0, tiled=True)  105 us
    unnamed x2, blocking collectives  79.6 us
    all_gather x2, blocking collectives, gather_layer(): lax.all_gather(bi_part, ('dp', 'fsdp'), axis=0, tiled=True)  71 us
  transfers between devices with their start and end apart: 16, of which 14 were waited for; matrix products, arithmetic and copies ran while one was open for 16% of the time, Pallas kernels for 0%

commit v1 on v0

v1 whole, which is shorter than its diff:
```python
import jax
import jax.numpy as jnp
from jax import lax
from jax.sharding import PartitionSpec as P

HEADS = 16
HEAD = 64
ROT = 32
LAYERS = 2
AXES = ("dp", "fsdp")

CORE_BIT = 0
PAIR_BIT = 2
FIRST_BIT = 3

layer_eps = 1e-05
gelu_scale = 0.7978845608028654
masked_fill = -1000000000.0
f32 = jnp.float32
bf16 = jnp.bfloat16


def gelu_tanh(values):
    return (
        0.5 * values * (1.0 + jnp.tanh(gelu_scale * (values + 0.044715 * values * values * values)))
    )


def gelu_slope(values):
    inner = jnp.tanh(gelu_scale * (values + 0.044715 * values * values * values))
    return 0.5 * (1.0 + inner) + 0.5 * values * (1.0 - inner * inner) * gelu_scale * (
        1.0 + 3.0 * 0.044715 * values * values
    )


def positions_of(segment_ids):
    last_axis = segment_ids.ndim - 1
    index_grid = lax.broadcasted_iota(jnp.int32, segment_ids.shape, last_axis)
    earlier = jnp.concatenate([segment_ids[..., :1] - 1, segment_ids[..., :-1]], axis=last_axis)
    starts = jnp.where(segment_ids != earlier, index_grid, jnp.zeros_like(index_grid))
    starts = lax.cummax(starts, axis=last_axis)
    return index_grid - starts


def attention_mask(segment_ids):
    length = segment_ids.shape[-1]
    row_index = lax.broadcasted_iota(jnp.int32, (length, length), 0)
    col_index = lax.broadcasted_iota(jnp.int32, (length, length), 1)
    same_doc = segment_ids[:, :, None] == segment_ids[:, None, :]
    return jnp.logical_and(same_doc, (col_index <= row_index)[None])


def rotary_tables(positions, rot_dim):
    half_rot = rot_dim // 2
    frequency = 10000.0 ** (-(jnp.arange(half_rot, dtype=jnp.float32) * 2.0 / rot_dim))
    angles = positions.astype(jnp.float32)[..., None] * frequency
    return (jnp.cos(angles), jnp.sin(angles))


def rotate(values, cosine, sine_table, rot_dim):
    half_rot = rot_dim // 2
    leading = values[..., :half_rot]
    trailing = values[..., half_rot:rot_dim]
    cos_heads = cosine[..., None, :]
    sin_heads = sine_table[..., None, :]
    return jnp.concatenate(
        [
            leading * cos_heads - trailing * sin_heads,
            trailing * cos_heads + leading * sin_heads,
            values[..., rot_dim:],
        ],
        axis=-1,
    )


def norm_stats(hidden):
    mean_value = jnp.mean(hidden, axis=-1, keepdims=True)
    centered = hidden - mean_value
    variance = jnp.mean(centered * centered, axis=-1, keepdims=True)
    scale = lax.rsqrt(variance + layer_eps)
    return centered * scale, scale


def build(mesh):
    count = mesh.shape["dp"] * mesh.shape["fsdp"]
    bits = count.bit_length() - 1
    head_bits = HEADS.bit_length() - 1
    every = list(range(bits - 1, -1, -1))
    shared = [b for b in every if b not in (CORE_BIT, PAIR_BIT)]
    others = [b for b in shared if b != FIRST_BIT]
    deep_order = [FIRST_BIT] + others[::-1]
    wide_order = [FIRST_BIT] + others
    unit_bits = wide_order[::-1]
    stands = list(range(bits))
    for share_bit, head_bit in ((PAIR_BIT, 1), (CORE_BIT, 3)):
        target = bits - head_bits + head_bit
        if target != share_bit:
            stands[share_bit], stands[target] = target, share_bit
    exchange = [
        (i, sum(((i >> stands[b]) & 1) << b for b in range(bits))) for i in range(count)
    ]
    head_order = [stands[b] for b in every if stands[b] not in (CORE_BIT, PAIR_BIT)]

    def program(
        tokens, segment_ids, cotangent, ln_gain, ln_bias, w_qkv, w_out, w_in, b_in, w_fo, b_fo
    ):
        device = lax.axis_index(AXES)
        seq_len, width = tokens.shape[1:]
        rows = w_qkv.shape[1]
        units = w_fo.shape[1]
        share_units = units * count // 4
        share_width = width // 4

        def bit(b):
            return ((device >> b) & 1) == 1

        def cross(value, b):
            return lax.ppermute(value, AXES, [(i, i ^ (1 << b)) for i in range(count)])

        def pair_up(mine, other, b):
            flag = bit(b)
            return jnp.stack([jnp.where(flag, other, mine), jnp.where(flag, mine, other)])

        def gather(value, order):
            for b in order:
                value = pair_up(value, cross(value, b), b)
            return value

        def arrange(value, have, want):
            rest = list(range(len(have), value.ndim))
            return value.transpose([have.index(b) for b in want] + rest)

        def half(value, axis, own, b):
            flag = bit(b)
            low = lax.index_in_dim(value, 0, axis, keepdims=False)
            high = lax.index_in_dim(value, 1, axis, keepdims=False)
            return jnp.where(flag, high, low) if own else jnp.where(flag, low, high)

        def fold(value, axis, b):
            arrived = cross(half(value, axis, False, b).astype(bf16), b)
            return half(value, axis, True, b).astype(f32) + arrived.astype(f32)

        def spread(value):
            pair = jnp.stack([value, cross(value, PAIR_BIT)])
            return jnp.concatenate([pair, cross(pair, CORE_BIT)]).reshape(-1, value.shape[-1])

        def collect(partial):
            parts = partial.reshape(2, 2, seq_len, width)
            kept = parts[0] + cross(parts[1].astype(bf16), CORE_BIT).astype(f32)
            return kept[0] + cross(kept[1].astype(bf16), PAIR_BIT).astype(f32)

        small = jnp.concatenate(
            [
                ln_gain.reshape(-1),
                ln_bias.reshape(-1),
                b_fo.reshape(-1),
                b_in.reshape(-1),
                segment_ids.astype(bf16).reshape(-1),
            ]
        )[None]
        for b in [CORE_BIT, PAIR_BIT] + deep_order:
            arrived = cross(small, b)
            flag = bit(b)
            small = jnp.concatenate(
                [jnp.where(flag, arrived, small), jnp.where(flag, small, arrived)]
            )
        small_bits = ([CORE_BIT, PAIR_BIT] + deep_order)[::-1]
        small = arrange(small.reshape([2] * bits + [-1]), small_bits, every).reshape(count, -1)
        span = LAYERS * rows

        def vector(offset, depth):
            first = offset * span + depth * rows
            return small[:, first : first + rows].reshape(-1).astype(f32)

        gains = [vector(0, depth) for depth in range(LAYERS)]
        shifts = [vector(1, depth) for depth in range(LAYERS)]
        out_shifts = [vector(2, depth) for depth in range(LAYERS)]

        def own_units(value):
            by_bit = value.reshape([2] * bits + [-1])
            have = list(every)
            for b in (PAIR_BIT, CORE_BIT):
                by_bit = half(by_bit, have.index(b), True, b)
                have.remove(b)
            return arrange(by_bit, have, unit_bits).reshape(-1)

        unit_shifts = [
            own_units(small[:, 3 * span + depth * units : 3 * span + (depth + 1) * units]).astype(
                f32
            )
            for depth in range(LAYERS)
        ]
        all_ids = small[:, 3 * span + LAYERS * units :].astype(jnp.int32)
        relative = [0, 1 << PAIR_BIT, 1 << CORE_BIT, (1 << PAIR_BIT) | (1 << CORE_BIT)]
        ids = jnp.concatenate(
            [lax.dynamic_slice_in_dim(all_ids, device ^ r, 1, 0) for r in relative]
        )
        cosine, sine_table = rotary_tables(positions_of(ids), ROT)
        allowed = attention_mask(ids)[:, None]

        def reach(columns):
            value = columns
            mine, away = half(value, 0, True, CORE_BIT), half(value, 0, False, CORE_BIT)
            value = pair_up(mine, cross(away, CORE_BIT), CORE_BIT)
            mine, away = half(value, 1, True, PAIR_BIT), half(value, 1, False, PAIR_BIT)
            value = pair_up(mine, cross(away, PAIR_BIT), PAIR_BIT)
            return value

        def deep(columns):
            value = gather(reach(columns), deep_order)
            have = deep_order[::-1] + [PAIR_BIT, CORE_BIT]
            return arrange(value, have, every).reshape(width, -1)

        def qkv_columns(value):
            parts = value.reshape(rows, 3, 2, 2, 2, 2 * HEAD)
            return parts.transpose(2, 4, 0, 1, 3, 5).reshape(2, 2, rows, 3 * share_width)

        def unit_columns(value):
            parts = value.reshape([rows] + [2] * bits + [units])
            where = {b: 1 + i for i, b in enumerate(every)}
            order = [where[CORE_BIT], where[PAIR_BIT], 0] + [where[b] for b in unit_bits]
            return parts.transpose(order + [bits + 1]).reshape(2, 2, rows, share_units)

        def fetch(depth):
            attn_in = deep(qkv_columns(w_qkv[depth]))
            mlp_in = deep(unit_columns(w_in[depth]))
            rows_out = lax.ppermute(w_out[depth], AXES, exchange)
            wide = gather(jnp.concatenate([w_fo[depth], rows_out]), wide_order)
            have = wide_order[::-1]
            mlp_back = arrange(wide[..., :units, :], have, unit_bits).reshape(share_units, width)
            attn_back = arrange(wide[..., units:, :], have, head_order).reshape(
                share_width, width
            )
            return attn_in, attn_back, mlp_in, mlp_back

        heads_shape = (4, seq_len, HEADS // 4, HEAD)
        scale = HEAD ** (-0.5)

        def scores_of(rot_query, rot_key):
            scores = (
                jnp.einsum("gshe,gthe->ghst", rot_query, rot_key, preferred_element_type=f32)
                * scale
            )
            return jnp.where(allowed, scores, masked_fill)

        def forward(hidden, weights, depth):
            attn_in, attn_back, mlp_in, mlp_back = weights
            centered, _ = norm_stats(hidden)
            normed = spread((centered * gains[depth] + shifts[depth]).astype(bf16))
            projected = jnp.dot(normed, attn_in, preferred_element_type=f32)
            query = projected[:, :share_width].reshape(heads_shape)
            key = projected[:, share_width : 2 * share_width].reshape(heads_shape)
            value_low = projected[:, 2 * share_width :].reshape(heads_shape).astype(bf16)
            rot_query = rotate(query, cosine, sine_table, ROT).astype(bf16)
            rot_key = rotate(key, cosine, sine_table, ROT).astype(bf16)
            scores = scores_of(rot_query, rot_key)
            row_max = jnp.max(scores, axis=-1, keepdims=True)
            exponent = jnp.exp(scores - row_max)
            row_total = jnp.sum(exponent, axis=-1, keepdims=True)
            probs = (exponent / row_total).astype(bf16)
            attended = jnp.einsum("ghst,gthe->gshe", probs, value_low, preferred_element_type=f32)
            attended = attended.reshape(4 * seq_len, share_width).astype(bf16)
            pre = jnp.dot(normed, mlp_in, preferred_element_type=f32) + unit_shifts[depth]
            act = gelu_tanh(pre).astype(bf16)
            partial = jnp.dot(attended, attn_back, preferred_element_type=f32) + jnp.dot(
                act, mlp_back, preferred_element_type=f32
            )
            kept = (
                hidden,
                normed,
                rot_query,
                rot_key,
                value_low,
                row_max,
                row_total,
                attended,
                pre,
                act,
            )
            return kept, hidden + collect(partial) + out_shifts[depth]

        def deliver_deep(left, right, restore):
            top, order = deep_order[-1], deep_order[::-1]
            size = width // 2
            begin = jnp.where(bit(top), size, 0)
            away = lax.dynamic_slice_in_dim(left, size - begin, size, 1)
            mine = lax.dynamic_slice_in_dim(left, begin, size, 1)
            sent = cross(jnp.dot(away.T, right, preferred_element_type=f32).astype(bf16), top)
            value = jnp.dot(mine.T, right, preferred_element_type=f32) + sent.astype(f32)
            have = [b for b in every if b != top]
            value = value.reshape([2] * len(have) + [rows, -1])
            for b in order[1:]:
                value = fold(value, have.index(b), b)
                have.remove(b)
            value = value.astype(bf16)
            arrived = cross(half(value, 0, False, PAIR_BIT), PAIR_BIT)
            value = pair_up(half(value, 0, True, PAIR_BIT), arrived, PAIR_BIT)
            arrived = cross(half(value, 1, False, CORE_BIT), CORE_BIT)
            value = pair_up(half(value, 1, True, CORE_BIT), arrived, CORE_BIT)
            return restore(value.astype(f32))

        def restore_qkv(value):
            parts = value.reshape(2, 2, rows, 3, 2, 2 * HEAD)
            return parts.transpose(2, 3, 0, 4, 1, 5).reshape(rows, 3 * width)

        def restore_units(value):
            parts = value.reshape([2, 2, rows] + [2] * len(unit_bits) + [units])
            where = {b: 3 + i for i, b in enumerate(unit_bits)}
            where[CORE_BIT], where[PAIR_BIT] = 0, 1
            order = [2] + [where[b] for b in every] + [parts.ndim - 1]
            return parts.transpose(order).reshape(rows, units * count)

        def deliver_wide(act, attended, grad_low):
            top, order = wide_order[-1], wide_order[::-1]
            size = share_units // 2
            begin = jnp.where(bit(top), size, 0)
            away = lax.dynamic_slice_in_dim(act, size - begin, size, 1)
            mine = lax.dynamic_slice_in_dim(act, begin, size, 1)
            have = unit_bits[1:]
            heads_part = jnp.dot(attended.T, grad_low, preferred_element_type=f32)
            heads_part = arrange(
                heads_part.reshape([2] * len(head_order) + [rows, width]), head_order, unit_bits
            )

            def whole(units_part, heads_half):
                units_part = units_part.reshape([2] * len(have) + [units, width])
                return jnp.concatenate([units_part, heads_half], axis=len(have))

            sent = whole(
                jnp.dot(away.T, grad_low, preferred_element_type=f32).astype(bf16),
                half(heads_part, 0, False, top).astype(bf16),
            )
            arrived = cross(sent, top)
            value = whole(
                jnp.dot(mine.T, grad_low, preferred_element_type=f32),
                half(heads_part, 0, True, top),
            ) + arrived.astype(f32)
            have = list(have)
            for b in order[1:]:
                value = fold(value, have.index(b), b)
                have.remove(b)
            rows_out = lax.ppermute(value[units:].astype(bf16), AXES, exchange).astype(f32)
            return value[:units], rows_out

        def backward(grad, weights, kept, depth):
            attn_in, attn_back, mlp_in, mlp_back = weights
            (
                hidden,
                normed,
                rot_query,
                rot_key,
                value_low,
                row_max,
                row_total,
                attended,
                pre,
                act,
            ) = kept
            own_low = grad.astype(bf16)
            d_shift_out = jnp.sum(own_low, axis=0, dtype=f32)
            grad_low = spread(own_low)
            d_fo, d_out = deliver_wide(act, attended, grad_low)
            d_act = jnp.dot(grad_low, mlp_back.T, preferred_element_type=f32)
            d_pre_wide = d_act * gelu_slope(pre)
            d_pre = d_pre_wide.astype(bf16)
            d_unit_shift = jnp.sum(d_pre, axis=0, dtype=f32)
            d_in = deliver_deep(normed, d_pre, restore_units)
            d_attended = (
                jnp.dot(grad_low, attn_back.T, preferred_element_type=f32)
                .astype(bf16)
                .reshape(heads_shape)
            )
            probs_full = jnp.exp(scores_of(rot_query, rot_key) - row_max) / row_total
            d_values = jnp.einsum(
                "ghst,gshe->gthe", probs_full.astype(bf16), d_attended, preferred_element_type=f32
            )
            d_probs = jnp.einsum(
                "gshe,gthe->ghst", d_attended, value_low, preferred_element_type=f32
            )
            row_dot = jnp.sum(probs_full * d_probs, axis=-1, keepdims=True)
            d_scores = (probs_full * (d_probs - row_dot)).astype(bf16)
            d_query = (
                jnp.einsum("ghst,gthe->gshe", d_scores, rot_key, preferred_element_type=f32) * scale
            )
            d_key = (
                jnp.einsum("ghst,gshe->gthe", d_scores, rot_query, preferred_element_type=f32)
                * scale
            )
            d_projected = jnp.concatenate(
                [
                    rotate(d_query, cosine, -sine_table, ROT).reshape(-1, share_width),
                    rotate(d_key, cosine, -sine_table, ROT).reshape(-1, share_width),
                    d_values.reshape(-1, share_width),
                ],
                axis=1,
            ).astype(bf16)
            d_qkv = deliver_deep(normed, d_projected, restore_qkv)
            partial = jnp.dot(d_projected, attn_in.T, preferred_element_type=f32) + jnp.dot(
                d_pre, mlp_in.T, preferred_element_type=f32
            )
            d_normed = collect(partial)
            centered, spread_scale = norm_stats(hidden)
            d_gain = jnp.sum(d_normed * centered, axis=0)
            d_shift = jnp.sum(d_normed, axis=0)
            d_centered = d_normed * gains[depth]
            grad = grad + spread_scale * (
                d_centered
                - jnp.mean(d_centered, axis=-1, keepdims=True)
                - centered * jnp.mean(d_centered * centered, axis=-1, keepdims=True)
            )
            return grad, (d_gain, d_shift, d_shift_out, d_unit_shift), (d_qkv, d_out, d_in, d_fo)

        hidden = tokens[0].astype(f32)
        saved, weights = [], []
        for depth in range(LAYERS):
            weights.append(fetch(depth))
            kept, hidden = forward(hidden, weights[depth], depth)
            saved.append(kept)
        layer_out = hidden.astype(bf16)[None]
        grad = cotangent[0].astype(f32)
        vectors, owned = [None] * LAYERS, [None] * LAYERS
        for depth in range(LAYERS - 1, -1, -1):
            grad, vectors[depth], owned[depth] = backward(
                grad, weights[depth], saved[depth], depth
            )

        def unit_rows(value):
            by_bit = value.reshape([2] * len(unit_bits) + [units])
            have = list(unit_bits)
            for b in (PAIR_BIT, CORE_BIT):
                zero = jnp.zeros_like(by_bit)
                flag = bit(b)
                by_bit = jnp.stack(
                    [jnp.where(flag, zero, by_bit), jnp.where(flag, by_bit, zero)]
                )
                have = [b] + have
            return arrange(by_bit, have, every).reshape(count, units)

        table = jnp.concatenate(
            [vectors[depth][kind].reshape(count, rows) for kind in range(3) for depth in range(LAYERS)]
            + [unit_rows(vectors[depth][3]) for depth in range(LAYERS)],
            axis=1,
        )
        have = list(every)
        table = table.reshape([2] * bits + [-1])
        for b in deep_order[::-1] + [PAIR_BIT, CORE_BIT]:
            axis = have.index(b)
            arrived = cross(half(table, axis, False, b), b)
            table = half(table, axis, True, b) + arrived
            have.remove(b)

        def own_vector(kind):
            return jnp.stack(
                [
                    table[(kind * LAYERS + depth) * rows : (kind * LAYERS + depth + 1) * rows]
                    for depth in range(LAYERS)
                ]
            )

        d_b_in = table[3 * span :].reshape(LAYERS, units)
        return (
            layer_out,
            grad[None],
            own_vector(0),
            own_vector(1),
            jnp.stack([owned[depth][0] for depth in range(LAYERS)]),
            jnp.stack([owned[depth][1] for depth in range(LAYERS)]),
            jnp.stack([owned[depth][2] for depth in range(LAYERS)]),
            d_b_in,
            jnp.stack([owned[depth][3] for depth in range(LAYERS)]),
            own_vector(2),
        )

    return program


def solution(mesh):
    batch = P(AXES, None, None)
    columns = P(None, AXES)
    matrix = P(None, AXES, None)
    return jax.shard_map(
        build(mesh),
        mesh=mesh,
        in_specs=(
            batch,
            P(AXES, None),
            batch,
            columns,
            columns,
            matrix,
            matrix,
            matrix,
            columns,
            matrix,
            columns,
        ),
        out_specs=(
            batch,
            batch,
            columns,
            columns,
            matrix,
            matrix,
            matrix,
            columns,
            matrix,
            columns,
        ),
        check_vma=False,
    )
```

time: 1980 us -> 716 us (0.36)
  waiting for transfers between devices: 1450 us -> 271 us
  blocking collectives: 151 us -> 0 us
  starting transfers between devices: 1.03 us -> 112 us
  matrix products: 175 us -> 79.4 us
  other arithmetic: 22.6 us -> 89.5 us
    reduce_scatter x8 -> x0, waiting for transfers between devices: 1080 us -> none  [the longest x2 373 us: scatter_layer(): lax.psum_scatter(flat[6], ('dp', 'fsdp'), scatter_dimension=0, tiled=True)]
    all_gather x8 -> x0, waiting for transfers between devices: 367 us -> none  [the longest x2 143 us: gather_layer(): lax.all_gather(wf_part, ('dp', 'fsdp'), axis=0, tiled=True)]
    ppermute x0 -> x82, waiting for transfers between devices: none -> 271 us  [the longest x78 271 us: cross(): return lax.ppermute(value, AXES, [(i, i ^ 1 << b) for i in range(count)])]
    ppermute x0 -> x82, starting transfers between devices: none -> 112 us  [the longest x78 106 us: cross(): return lax.ppermute(value, AXES, [(i, i ^ 1 << b) for i in range(count)])]
    dot_general x34 -> x40, matrix products: 165 us -> 69.6 us  [the longest x2 10.4 us: backward(): d_act = jnp.dot(grad_low, mlp_back.T, preferred_element_type=f32)]
    reshape x8 -> x20, local copies, waits for them, and re-layouts: 110 us -> 25.9 us  [the longest x6 7.41 us: program(): vectors[depth][kind].reshape(count, rows)]
    unnamed x2 -> x0, blocking collectives: 79.6 us -> none
    all_gather x2 -> x0, blocking collectives: 71 us -> none  [gather_layer(): lax.all_gather(bi_part, ('dp', 'fsdp'), axis=0, tiled=True)]
  transfers between devices with their start and end apart: 16 -> 82, of which waited for: 14 -> 29; matrix products, arithmetic and copies ran while one was open for 16% -> 31% of each run, Pallas kernels for 0% -> 0%
where the time goes in v1:
time: 716 us; the launch traced here: 702 us
  waiting for transfers between devices  271 us (38%)
  local copies, waits for them, and re-layouts  146 us (20%)
  starting transfers between devices  112 us (16%)
  other arithmetic  89.5 us (12%)
  matrix products  79.4 us (11%)
    ppermute x78, waiting for transfers between devices, cross(): return lax.ppermute(value, AXES, [(i, i ^ 1 << b) for i in range(count)])  271 us
    ppermute x78, starting transfers between devices, cross(): return lax.ppermute(value, AXES, [(i, i ^ 1 << b) for i in range(count)])  106 us
    unnamed x262, local copies, waits for them, and re-layouts  46.7 us
    another operation x50, other arithmetic, pair_up(): jnp.stack([jnp.where(flag, other, mine), jnp.where(flag, mine, other)])  20.5 us
    slice x4, local copies, waits for them, and re-layouts, rotate(): trailing = values[..., half_rot:rot_dim]  15 us
  transfers between devices with their start and end apart: 82, of which 29 were waited for; matrix products, arithmetic and copies ran while one was open for 31% of the time, Pallas kernels for 0%

profile of v1, /device:TPU:19, one launch (start us, length us, event | category | flops | bytes accessed | tf_op | source)
XLA Modules:
  0.0 701.7 jit_solution(8716082875598986885)
XLA Ops:
  20.1 3.3 collective-permute-done.2
  28.9 5.1 collective-permute-start.34
  49.0 32.9 %collective-permute-done.26 = bf16[2,32,768]{2,1,0:T(8,128)(2,1)S(1)} collective-permute-done((bf16[2,32,768]{2,1,0:T(8,128)(2,1)S(1)}, bf16[2,32,768]{2,1,0:T(8,128)(2,1)S(1)}, u32[]{:S(2)}, u32[]{:S(2)}) %collective-permute-start.26) | collective-permute-done | bytes 98336 | tf_op jit(solution)/shard_map/ppermute | solution.py:118
  90.6 3.0 collective-permute-done.17
  93.8 6.0 collective-permute-done.9
  100.6 8.6 %collective-permute-done.27 = bf16[2,2,32,768]{3,2,1,0:T(8,128)(2,1)S(1)} collective-permute-done((bf16[2,2,32,768]{3,2,1,0:T(8,128)(2,1)S(1)}, bf16[2,2,32,768]{3,2,1,0:T(8,128)(2,1)S(1)}, u32[]{:S(2)}, u32[]{:S(2)}) %collective-permute-start.27) | collective-permute-done | bytes 196640 | tf_op jit(solution)/shard_map/ppermute | solution.py:118
  109.3 2.8 collective-permute-start.18
  115.7 18.4 %collective-permute-done.36 = bf16[2,2,32,1024]{3,2,1,0:T(8,128)(2,1)S(1)} collective-permute-done((bf16[2,2,32,1024]{3,2,1,0:T(8,128)(2,1)S(1)}, bf16[2,2,32,1024]{3,2,1,0:T(8,128)(2,1)S(1)}, u32[]{:S(2)}, u32[]{:S(2)}) %collective-permute-start.36) | collective-permute-done | bytes 262176 | tf_op jit(solution)/shard_map/ppermute | solution.py:118
  139.5 6.7 collective-permute-start.6
  146.3 5.6 collective-permute-done.19
  155.5 22.2 %collective-permute-done.11 = bf16[2,2,2,2,32,768]{5,4,3,0,2,1:T(8,128)(2,1)S(1)} collective-permute-done((bf16[2,2,2,2,32,768]{5,4,3,0,2,1:T(8,128)(2,1)S(1)}, bf16[2,2,2,2,32,768]{5,4,3,0,2,1:T(8,128)(2,1)S(1)}, u32[]{:S(2)}, u32[]{:S(2)}) %collective-permute-start.11) | collective-permute-done | bytes 786464 | tf_op jit(solution)/shard_map/ppermute | solution.py:118
  185.7 3.1 reshape.850
  188.8 5.4 fusion.164
  199.2 3.2 fusion.163
  204.9 3.0 copy.346
  214.6 2.8 reshape.848
  221.3 5.0 fusion.168
  230.2 10.2 %collective-permute-start.42 = (bf16[2,256,1024]{2,1,0:T(8,128)(2,1)S(1)}, bf16[2,256,1024]{2,1,0:T(8,128)(2,1)S(1)}, u32[]{:S(2)}, u32[]{:S(2)}) collective-permute-start(bf16[2,256,1024]{2,1,0:T(8,128)(2,1)S(1)} %copy-done.77), channel_id=1, source_target_pairs={{0,1},{1,0},{2,3},{3,2},{4,5},{5,4},{6,7},{7,6},{8,9},{9,8},{10,11... | collective-permute-start | bytes 3145736 | tf_op jit(solution)/shard_map/ppermute | solution.py:118
  244.1 5.0 multiply_convert_fusion.3
  264.2 11.9 %collective-permute-done.29 = bf16[2,2,2,2,32,768]{5,4,3,2,1,0:T(8,128)(2,1)S(1)} collective-permute-done((bf16[2,2,2,2,32,768]{5,4,3,2,1,0:T(8,128)(2,1)S(1)}, bf16[2,2,2,2,32,768]{5,4,3,2,1,0:T(8,128)(2,1)S(1)}, u32[]{:S(2)}, u32[]{:S(2)}) %collective-permute-start.29) | collective-permute-done | bytes 786464 | tf_op jit(solution)/shard_map/ppermute | solution.py:118
  278.6 20.0 %collective-permute-done.38 = bf16[2,2,2,2,32,1024]{5,4,3,2,1,0:T(8,128)(2,1)S(1)} collective-permute-done((bf16[2,2,2,2,32,1024]{5,4,3,2,1,0:T(8,128)(2,1)S(1)}, bf16[2,2,2,2,32,1024]{5,4,3,2,1,0:T(8,128)(2,1)S(1)}, u32[]{:S(2)}, u32[]{:S(2)}) %collective-permute-start.38) | collective-permute-done | bytes 1048608 | tf_op jit(solution)/shard_map/ppermute | solution.py:118
  307.7 2.8 reshape.854
  312.7 2.9 pad_maximum_fusion
  325.3 3.1 fusion.162
  332.1 3.2 fusion.161
  351.2 4.8 fusion.169
  356.1 3.1 fusion.38
  369.2 3.6 multiply_convert_fusion.2
  372.8 5.1 convert_reduce_fusion
  397.9 12.6 %collective-permute-done.59 = bf16[512,768]{1,0:T(8,128)(2,1)S(1)} collective-permute-done((bf16[512,768]{1,0:T(8,128)(2,1)S(1)}, bf16[512,768]{1,0:T(8,128)(2,1)S(1)}, u32[]{:S(2)}, u32[]{:S(2)}) %collective-permute-start.59) | collective-permute-done | bytes 786464 | tf_op jit(solution)/shard_map/ppermute | solution.py:118
  414.9 18.0 %collective-permute-done.77 = bf16[512,1024]{1,0:T(8,128)(2,1)S(1)} collective-permute-done((bf16[512,1024]{1,0:T(8,128)(2,1)S(1)}, bf16[512,1024]{1,0:T(8,128)(2,1)S(1)}, u32[]{:S(2)}, u32[]{:S(2)}) %collective-permute-start.77) | collective-permute-done | bytes 1048608 | tf_op jit(solution)/shard_map/ppermute | solution.py:118
  436.7 3.2 collective-permute-start.61
  440.7 3.8 collective-permute-done.61
  448.6 6.7 collective-permute-done.62
  471.2 4.3 collective-permute-start.79
  477.7 8.5 %collective-permute-done.79 = bf16[2,2,32,1024]{3,2,1,0:T(8,128)(2,1)S(1)} collective-permute-done((bf16[2,2,32,1024]{3,2,1,0:T(8,128)(2,1)S(1)}, bf16[2,2,32,1024]{3,2,1,0:T(8,128)(2,1)S(1)}, u32[]{:S(2)}, u32[]{:S(2)}) %collective-permute-start.79) | collective-permute-done | bytes 262176 | tf_op jit(solution)/shard_map/ppermute | solution.py:118
  488.0 3.9 convert_reduce_fusion.4
  502.0 7.6 %collective-permute-done.45 = bf16[256,1024]{1,0:T(8,128)(2,1)S(1)} collective-permute-done((bf16[256,1024]{1,0:T(8,128)(2,1)}, bf16[256,1024]{1,0:T(8,128)(2,1)S(1)}, u32[]{:S(2)}, u32[]{:S(2)}) %collective-permute-start.45) | collective-permute-done | bytes 524320 | tf_op jit(solution)/shard_map/ppermute | solution.py:118
  516.8 13.4 %collective-permute-done.70 = bf16[160,1024]{1,0:T(8,128)(2,1)} collective-permute-done((bf16[160,1024]{1,0:T(8,128)(2,1)}, bf16[160,1024]{1,0:T(8,128)(2,1)}, u32[]{:S(2)}, u32[]{:S(2)}) %collective-permute-start.70) | collective-permute-done | bytes 327712 | tf_op jit(solution)/shard_map/ppermute | solution.py:118
  540.2 3.1 fusion.39
  555.4 5.3 convert_reduce_fusion.1
  573.6 8.9 %collective-permute-done.54 = bf16[512,768]{1,0:T(8,128)(2,1)S(1)} collective-permute-done((bf16[512,768]{1,0:T(8,128)(2,1)S(1)}, bf16[512,768]{1,0:T(8,128)(2,1)S(1)}, u32[]{:S(2)}, u32[]{:S(2)}) %collective-permute-start.54) | collective-permute-done | bytes 786464 | tf_op jit(solution)/shard_map/ppermute | solution.py:118
  584.3 20.6 %collective-permute-done.72 = bf16[512,1024]{1,0:T(8,128)(2,1)S(1)} collective-permute-done((bf16[512,1024]{1,0:T(8,128)(2,1)S(1)}, bf16[512,1024]{1,0:T(8,128)(2,1)S(1)}, u32[]{:S(2)}, u32[]{:S(2)}) %collective-permute-start.72) | collective-permute-done | bytes 1048608 | tf_op jit(solution)/shard_map/ppermute | solution.py:118
  613.1 14.0 %collective-permute-done.56 = bf16[2,2,32,768]{3,2,1,0:T(8,128)(2,1)S(1)} collective-permute-done((bf16[2,2,32,768]{3,2,1,0:T(8,128)(2,1)S(1)}, bf16[2,2,32,768]{3,2,1,0:T(8,128)(2,1)S(1)}, u32[]{:S(2)}, u32[]{:S(2)}) %collective-permute-start.56) | collective-permute-done | bytes 196640 | tf_op jit(solution)/shard_map/ppermute | solution.py:118
  630.9 3.0 collective-permute-start.58
  663.5 3.7 collective-permute-start.53
  667.1 2.9 fusion.46
  685.8 12.2 %collective-permute-done.66 = bf16[160,1024]{1,0:T(8,128)(2,1)S(1)} collective-permute-done((bf16[160,1024]{1,0:T(8,128)(2,1)S(1)}, bf16[160,1024]{1,0:T(8,128)(2,1)S(1)}, u32[]{:S(2)}, u32[]{:S(2)}) %collective-permute-start.66) | collective-permute-done | bytes 327712 | tf_op jit(solution)/shard_map/ppermute | solution.py:118
  (760 shorter events, 329.4 us)
Async XLA Ops:
  6.6 34.8 %collective-permute-start.30 = (bf16[32,1024]{1,0:T(8,128)(2,1)}, bf16[32,1024]{1,0:T(8,128)(2,1)S(1)}, u32[]{:S(2)}, u32[]{:S(2)}) collective-permute-start(bf16[32,1024]{1,0:T(8,128)(2,1)} %get-tuple-element.141), channel_id=1, source_target_pairs={{0,0},{1,16},{2,2},{3,18},{4,4},{5,20},{6,6},{7,22},{8,8},{9,24},{... | collective-permute-start | bytes 196616 | tf_op jit(solution)/shard_map/ppermute | solution.py:227
  8.3 33.2 %collective-permute-start.12 = (bf16[32,1024]{1,0:T(8,128)(2,1)}, bf16[32,1024]{1,0:T(8,128)(2,1)S(1)}, u32[]{:S(2)}, u32[]{:S(2)}) collective-permute-start(bf16[32,1024]{1,0:T(8,128)(2,1)} %get-tuple-element.142), channel_id=1, source_target_pairs={{0,0},{1,16},{2,2},{3,18},{4,4},{5,20},{6,6},{7,22},{8,8},{9,24},{... | collective-permute-start | bytes 196616 | tf_op jit(solution)/shard_map/ppermute | solution.py:227
  11.9 31.0 %collective-permute-start.25 = (bf16[2,32,768]{2,1,0:T(8,128)(2,1)}, bf16[2,32,768]{2,1,0:T(8,128)(2,1)}, u32[]{:S(2)}, u32[]{:S(2)}) collective-permute-start(bf16[2,32,768]{2,1,0:T(8,128)(2,1)} %select_n.1211), channel_id=1, source_target_pairs={{0,1},{1,0},{2,3},{3,2},{4,5},{5,4},{6,7},{7,6},{8,9},{9,8},{10,11... | collective-permute-start | bytes 294920 | tf_op jit(solution)/shard_map/ppermute | solution.py:118
  15.6 28.5 %collective-permute-start.7 = (bf16[2,32,768]{2,1,0:T(8,128)(2,1)}, bf16[2,32,768]{2,1,0:T(8,128)(2,1)}, u32[]{:S(2)}, u32[]{:S(2)}) collective-permute-start(bf16[2,32,768]{2,1,0:T(8,128)(2,1)} %select_n.1148), channel_id=1, source_target_pairs={{0,1},{1,0},{2,3},{3,2},{4,5},{5,4},{6,7},{7,6},{8,9},{9,8},{10,11... | collective-permute-start | bytes 294920 | tf_op jit(solution)/shard_map/ppermute | solution.py:118
  41.5 95.2 %collective-permute-start.41 = (bf16[256,1024]{1,0:T(8,128)(2,1)S(1)}, bf16[256,1024]{1,0:T(8,128)(2,1)S(1)}, u32[]{:S(2)}, u32[]{:S(2)}) collective-permute-start(bf16[256,1024]{1,0:T(8,128)(2,1)S(1)} %bitcast.832), channel_id=1, source_target_pairs={{0,4},{1,5},{2,6},{3,7},{4,0},{5,1},{6,2},{7,3},{8,12},{9,13},{10,... | collective-permute-start | bytes 1572872 | tf_op jit(solution)/shard_map/ppermute | solution.py:118
  42.9 96.2 %collective-permute-start.5 = (bf16[256,1024]{1,0:T(8,128)(2,1)}, bf16[256,1024]{1,0:T(8,128)(2,1)S(1)}, u32[]{:S(2)}, u32[]{:S(2)}) collective-permute-start(bf16[256,1024]{1,0:T(8,128)(2,1)} %fusion.41), channel_id=1, source_target_pairs={{0,4},{1,5},{2,6},{3,7},{4,0},{5,1},{6,2},{7,3},{8,12},{9,13},{10,... | collective-permute-start | bytes 1572872 | tf_op jit(solution)/shard_map/ppermute | solution.py:118
  44.1 68.1 %collective-permute-start.13 = (bf16[160,1024]{1,0:T(8,128)(2,1)S(1)}, bf16[160,1024]{1,0:T(8,128)(2,1)S(1)}, u32[]{:S(2)}, u32[]{:S(2)}) collective-permute-start(bf16[160,1024]{1,0:T(8,128)(2,1)S(1)} %pad_maximum_fusion.36), channel_id=1, source_target_pairs={{0,8},{1,9},{2,10},{3,11},{4,12},{5,13},{6,14},{7,15},{8,0},{9,1},... | collective-permute-start | bytes 983048 | tf_op jit(solution)/shard_map/ppermute | solution.py:118
  45.2 67.2 %collective-permute-start.31 = (bf16[160,1024]{1,0:T(8,128)(2,1)S(1)}, bf16[160,1024]{1,0:T(8,128)(2,1)S(1)}, u32[]{:S(2)}, u32[]{:S(2)}) collective-permute-start(bf16[160,1024]{1,0:T(8,128)(2,1)S(1)} %pad_maximum_fusion.37), channel_id=1, source_target_pairs={{0,8},{1,9},{2,10},{3,11},{4,12},{5,13},{6,14},{7,15},{8,0},{9,1},... | collective-permute-start | bytes 983048 | tf_op jit(solution)/shard_map/ppermute | solution.py:118
  47.6 34.3 %collective-permute-start.26 = (bf16[2,32,768]{2,1,0:T(8,128)(2,1)S(1)}, bf16[2,32,768]{2,1,0:T(8,128)(2,1)S(1)}, u32[]{:S(2)}, u32[]{:S(2)}) collective-permute-start(bf16[2,32,768]{2,1,0:T(8,128)(2,1)S(1)} %select_bitcast_fusion.50), channel_id=1, source_target_pairs={{0,4},{1,5},{2,6},{3,7},{4,0},{5,1},{6,2},{7,3},{8,12},{9,13},{10,... | collective-permute-start | bytes 294920 | tf_op jit(solution)/shard_map/ppermute | solution.py:118
  109.3 27.1 %collective-permute-start.18 = (bf16[2,2,32,1024]{3,2,1,0:T(8,128)(2,1)S(1)}, bf16[2,2,32,1024]{3,2,1,0:T(8,128)(2,1)S(1)}, u32[]{:S(2)}, u32[]{:S(2)}) collective-permute-start(bf16[2,2,32,1024]{3,2,1,0:T(8,128)(2,1)S(1)} %pad_maximum_fusion.38), channel_id=1, source_target_pairs={{0,8},{1,9},{2,10},{3,11},{4,12},{5,13},{6,14},{7,15},{8,0},{9,1},... | collective-permute-start | bytes 786440 | tf_op jit(solution)/shard_map/ppermute | solution.py:118
  112.2 22.0 %collective-permute-start.36 = (bf16[2,2,32,1024]{3,2,1,0:T(8,128)(2,1)S(1)}, bf16[2,2,32,1024]{3,2,1,0:T(8,128)(2,1)S(1)}, u32[]{:S(2)}, u32[]{:S(2)}) collective-permute-start(bf16[2,2,32,1024]{3,2,1,0:T(8,128)(2,1)S(1)} %pad_maximum_fusion.39), channel_id=1, source_target_pairs={{0,8},{1,9},{2,10},{3,11},{4,12},{5,13},{6,14},{7,15},{8,0},{9,1},... | collective-permute-start | bytes 786440 | tf_op jit(solution)/shard_map/ppermute | solution.py:118
  112.4 27.0 %collective-permute-start.10 = (bf16[2,2,2,32,768]{4,3,2,1,0:T(8,128)(2,1)S(1)}, bf16[2,2,2,32,768]{4,3,2,1,0:T(8,128)(2,1)S(1)}, u32[]{:S(2)}, u32[]{:S(2)}) collective-permute-start(bf16[2,2,2,32,768]{4,3,2,1,0:T(8,128)(2,1)S(1)} %pad_maximum_fusion.34), channel_id=1, source_target_pairs={{0,2},{1,3},{2,0},{3,1},{4,6},{5,7},{6,4},{7,5},{8,10},{9,11},{10,... | collective-permute-start | bytes 1179656 | tf_op jit(solution)/shard_map/ppermute | solution.py:118
  134.2 121.7 %collective-permute-start.28 = (bf16[2,2,2,32,768]{4,3,2,1,0:T(8,128)(2,1)}, bf16[2,2,2,32,768]{4,3,2,1,0:T(8,128)(2,1)}, u32[]{:S(2)}, u32[]{:S(2)}) collective-permute-start(bf16[2,2,2,32,768]{4,3,2,1,0:T(8,128)(2,1)} %pad_maximum_fusion.35), channel_id=1, source_target_pairs={{0,2},{1,3},{2,0},{3,1},{4,6},{5,7},{6,4},{7,5},{8,10},{9,11},{10,... | collective-permute-start | bytes 1179656 | tf_op jit(solution)/shard_map/ppermute | solution.py:118
  136.4 17.5 %collective-permute-start.14 = (bf16[2,160,1024]{2,1,0:T(8,128)(2,1)S(1)}, bf16[2,160,1024]{2,1,0:T(8,128)(2,1)S(1)}, u32[]{:S(2)}, u32[]{:S(2)}) collective-permute-start(bf16[2,160,1024]{2,1,0:T(8,128)(2,1)S(1)} %pad_maximum_fusion.21), channel_id=1, source_target_pairs={{0,16},{1,17},{2,18},{3,19},{4,20},{5,21},{6,22},{7,23},{8,24},{9,... | collective-permute-start | bytes 1966088 | tf_op jit(solution)/shard_map/ppermute | solution.py:118
  136.7 123.5 %collective-permute-start.32 = (bf16[2,160,1024]{2,1,0:T(8,128)(2,1)}, bf16[2,160,1024]{2,1,0:T(8,128)(2,1)}, u32[]{:S(2)}, u32[]{:S(2)}) collective-permute-start(bf16[2,160,1024]{2,1,0:T(8,128)(2,1)} %pad_maximum_fusion.22), channel_id=1, source_target_pairs={{0,16},{1,17},{2,18},{3,19},{4,20},{5,21},{6,22},{7,23},{8,24},{9,... | collective-permute-start | bytes 1966088 | tf_op jit(solution)/shard_map/ppermute | solution.py:118
  139.5 38.8 %collective-permute-start.6 = (bf16[2,256,1024]{2,1,0:T(8,128)(2,1)S(1)}, bf16[2,256,1024]{2,1,0:T(8,128)(2,1)S(1)}, u32[]{:S(2)}, u32[]{:S(2)}) collective-permute-start(bf16[2,256,1024]{2,1,0:T(8,128)(2,1)S(1)} %pad_maximum_fusion.12), channel_id=1, source_target_pairs={{0,1},{1,0},{2,3},{3,2},{4,5},{5,4},{6,7},{7,6},{8,9},{9,8},{10,11... | collective-permute-start | bytes 3145736 | tf_op jit(solution)/shard_map/ppermute | solution.py:118
  151.9 25.9 %collective-permute-start.11 = (bf16[2,2,2,2,32,768]{5,4,3,0,2,1:T(8,128)(2,1)S(1)}, bf16[2,2,2,2,32,768]{5,4,3,0,2,1:T(8,128)(2,1)S(1)}, u32[]{:S(2)}, u32[]{:S(2)}) collective-permute-start(bf16[2,2,2,2,32,768]{5,4,3,0,2,1:T(8,128)(2,1)S(1)} %pad_maximum_fusion.19), channel_id=1, source_target_pairs={{0,16},{1,17},{2,18},{3,19},{4,20},{5,21},{6,22},{7,23},{8,24},{9,... | collective-permute-start | bytes 2359304 | tf_op jit(solution)/shard_map/ppermute | solution.py:118
  154.0 104.7 %collective-permute-start.37 = (bf16[2,2,2,32,1024]{4,3,2,1,0:T(8,128)(2,1)}, bf16[2,2,2,32,1024]{4,3,2,1,0:T(8,128)(2,1)}, u32[]{:S(2)}, u32[]{:S(2)}) collective-permute-start(bf16[2,2,2,32,1024]{4,3,2,1,0:T(8,128)(2,1)} %pad_maximum_fusion.29), channel_id=1, source_target_pairs={{0,2},{1,3},{2,0},{3,1},{4,6},{5,7},{6,4},{7,5},{8,10},{9,11},{10,... | collective-permute-start | bytes 1572872 | tf_op jit(solution)/shard_map/ppermute | solution.py:118
  177.8 51.8 %collective-permute-start.20 = (bf16[2,2,2,2,32,1024]{5,4,3,0,2,1:T(8,128)(2,1)}, bf16[2,2,2,2,32,1024]{5,4,3,0,2,1:T(8,128)(2,1)}, u32[]{:S(2)}, u32[]{:S(2)}) collective-permute-start(bf16[2,2,2,2,32,1024]{5,4,3,0,2,1:T(8,128)(2,1)} %pad_maximum_fusion.13), channel_id=1, source_target_pairs={{0,16},{1,17},{2,18},{3,19},{4,20},{5,21},{6,22},{7,23},{8,24},{9,... | collective-permute-start | bytes 3145736 | tf_op jit(solution)/shard_map/ppermute | solution.py:118
  178.3 70.9 %collective-permute-start.15 = (bf16[2,2,160,1024]{3,2,0,1:T(8,128)(2,1)}, bf16[2,2,160,1024]{3,2,0,1:T(8,128)(2,1)}, u32[]{:S(2)}, u32[]{:S(2)}) collective-permute-start(bf16[2,2,160,1024]{3,2,0,1:T(8,128)(2,1)} %pad_maximum_fusion.8), channel_id=1, source_target_pairs={{0,2},{1,3},{2,0},{3,1},{4,6},{5,7},{6,4},{7,5},{8,10},{9,11},{10,... | collective-permute-start | bytes 3932168 | tf_op jit(solution)/shard_map/ppermute | solution.py:118
  230.2 33.2 %collective-permute-start.42 = (bf16[2,256,1024]{2,1,0:T(8,128)(2,1)S(1)}, bf16[2,256,1024]{2,1,0:T(8,128)(2,1)S(1)}, u32[]{:S(2)}, u32[]{:S(2)}) collective-permute-start(bf16[2,256,1024]{2,1,0:T(8,128)(2,1)S(1)} %copy-done.77), channel_id=1, source_target_pairs={{0,1},{1,0},{2,3},{3,2},{4,5},{5,4},{6,7},{7,6},{8,9},{9,8},{10,11... | collective-permute-start | bytes 3145736 | tf_op jit(solution)/shard_map/ppermute | solution.py:118
  257.4 18.7 %collective-permute-start.29 = (bf16[2,2,2,2,32,768]{5,4,3,2,1,0:T(8,128)(2,1)S(1)}, bf16[2,2,2,2,32,768]{5,4,3,2,1,0:T(8,128)(2,1)S(1)}, u32[]{:S(2)}, u32[]{:S(2)}) collective-permute-start(bf16[2,2,2,2,32,768]{5,4,3,2,1,0:T(8,128)(2,1)S(1)} %pad_maximum_fusion.20), channel_id=1, source_target_pairs={{0,16},{1,17},{2,18},{3,19},{4,20},{5,21},{6,22},{7,23},{8,24},{9,... | collective-permute-start | bytes 2359304 | tf_op jit(solution)/shard_map/ppermute | solution.py:118
  259.9 38.7 %collective-permute-start.38 = (bf16[2,2,2,2,32,1024]{5,4,3,2,1,0:T(8,128)(2,1)S(1)}, bf16[2,2,2,2,32,1024]{5,4,3,2,1,0:T(8,128)(2,1)S(1)}, u32[]{:S(2)}, u32[]{:S(2)}) collective-permute-start(bf16[2,2,2,2,32,1024]{5,4,3,2,1,0:T(8,128)(2,1)S(1)} %pad_maximum_fusion.15), channel_id=1, source_target_pairs={{0,16},{1,17},{2,18},{3,19},{4,20},{5,21},{6,22},{7,23},{8,24},{9,... | collective-permute-start | bytes 3145736 | tf_op jit(solution)/shard_map/ppermute | solution.py:118
  261.6 42.5 %collective-permute-start.33 = (bf16[2,2,160,1024]{3,2,1,0:T(8,128)(2,1)S(1)}, bf16[2,2,160,1024]{3,2,1,0:T(8,128)(2,1)S(1)}, u32[]{:S(2)}, u32[]{:S(2)}) collective-permute-start(bf16[2,2,160,1024]{3,2,1,0:T(8,128)(2,1)S(1)} %pad_maximum_fusion.9), channel_id=1, source_target_pairs={{0,2},{1,3},{2,0},{3,1},{4,6},{5,7},{6,4},{7,5},{8,10},{9,11},{10,... | collective-permute-start | bytes 3932168 | tf_op jit(solution)/shard_map/ppermute | solution.py:118
  278.5 22.1 %collective-permute-start.23 = (bf16[256,1024]{1,0:T(8,128)(2,1)S(1)}, bf16[256,1024]{1,0:T(8,128)(2,1)S(1)}, u32[]{:S(2)}, u32[]{:S(2)}) collective-permute-start(bf16[256,1024]{1,0:T(8,128)(2,1)S(1)} %add_convert_fusion), channel_id=1, source_target_pairs={{0,4},{1,5},{2,6},{3,7},{4,0},{5,1},{6,2},{7,3},{8,12},{9,13},{10,... | collective-permute-start | bytes 1572872 | tf_op jit(solution)/shard_map/ppermute | solution.py:118
  391.2 19.2 %collective-permute-start.59 = (bf16[512,768]{1,0:T(8,128)(2,1)S(1)}, bf16[512,768]{1,0:T(8,128)(2,1)S(1)}, u32[]{:S(2)}, u32[]{:S(2)}) collective-permute-start(bf16[512,768]{1,0:T(8,128)(2,1)S(1)} %convolution_convert_fusion.4), channel_id=1, source_target_pairs={{0,16},{1,17},{2,18},{3,19},{4,20},{5,21},{6,22},{7,23},{8,24},{9,... | collective-permute-start | bytes 2359304 | tf_op jit(solution)/shard_map/ppermute | solution.py:118
  394.4 18.6 %collective-permute-start.39 = (bf16[2,256,1024]{2,1,0:T(8,128)(2,1)S(1)}, bf16[2,256,1024]{2,1,0:T(8,128)(2,1)S(1)}, u32[]{:S(2)}, u32[]{:S(2)}) collective-permute-start(bf16[2,256,1024]{2,1,0:T(8,128)(2,1)S(1)} %bitcast.910), channel_id=1, source_target_pairs={{0,1},{1,0},{2,3},{3,2},{4,5},{5,4},{6,7},{7,6},{8,9},{9,8},{10,11... | collective-permute-start | bytes 3145736 | tf_op jit(solution)/shard_map/ppermute | solution.py:118
  394.8 38.2 %collective-permute-start.77 = (bf16[512,1024]{1,0:T(8,128)(2,1)S(1)}, bf16[512,1024]{1,0:T(8,128)(2,1)S(1)}, u32[]{:S(2)}, u32[]{:S(2)}) collective-permute-start(bf16[512,1024]{1,0:T(8,128)(2,1)S(1)} %convolution_convert_fusion), channel_id=1, source_target_pairs={{0,16},{1,17},{2,18},{3,19},{4,20},{5,21},{6,22},{7,23},{8,24},{9,... | collective-permute-start | bytes 3145736 | tf_op jit(solution)/shard_map/ppermute | solution.py:118
  395.0 41.2 %collective-permute-start.43 = (bf16[2,256,1024]{2,1,0:T(8,128)(2,1)S(1)}, bf16[2,256,1024]{2,1,0:T(8,128)(2,1)S(1)}, u32[]{:S(2)}, u32[]{:S(2)}) collective-permute-start(bf16[2,256,1024]{2,1,0:T(8,128)(2,1)S(1)} %bitcast.908), channel_id=1, source_target_pairs={{0,1},{1,0},{2,3},{3,2},{4,5},{5,4},{6,7},{7,6},{8,9},{9,8},{10,11... | collective-permute-start | bytes 3145736 | tf_op jit(solution)/shard_map/ppermute | solution.py:118
  395.6 51.0 %collective-permute-start.68 = (bf16[2,2,160,1024]{3,2,1,0:T(8,128)(2,1)S(1)}, bf16[2,2,160,1024]{3,2,1,0:T(8,128)(2,1)S(1)}, u32[]{:S(2)}, u32[]{:S(2)}) collective-permute-start(bf16[2,2,160,1024]{3,2,1,0:T(8,128)(2,1)S(1)} %pad_maximum_fusion.11), channel_id=1, source_target_pairs={{0,2},{1,3},{2,0},{3,1},{4,6},{5,7},{6,4},{7,5},{8,10},{9,11},{10,... | collective-permute-start | bytes 3932168 | tf_op jit(solution)/shard_map/ppermute | solution.py:118
  412.0 24.5 %collective-permute-start.60 = (bf16[2,2,2,32,768]{4,3,2,1,0:T(8,128)(2,1)S(1)}, bf16[2,2,2,32,768]{4,3,2,1,0:T(8,128)(2,1)S(1)}, u32[]{:S(2)}, u32[]{:S(2)}) collective-permute-start(bf16[2,2,2,32,768]{4,3,2,1,0:T(8,128)(2,1)S(1)} %fusion.89), channel_id=1, source_target_pairs={{0,2},{1,3},{2,0},{3,1},{4,6},{5,7},{6,4},{7,5},{8,10},{9,11},{10,... | collective-permute-start | bytes 1179656 | tf_op jit(solution)/shard_map/ppermute | solution.py:118
  414.4 73.6 %collective-permute-start.40 = (bf16[256,1024]{1,0:T(8,128)(2,1)}, bf16[256,1024]{1,0:T(8,128)(2,1)}, u32[]{:S(2)}, u32[]{:S(2)}) collective-permute-start(bf16[256,1024]{1,0:T(8,128)(2,1)} %fusion.81), channel_id=1, source_target_pairs={{0,4},{1,5},{2,6},{3,7},{4,0},{5,1},{6,2},{7,3},{8,12},{9,13},{10,... | collective-permute-start | bytes 1572872 | tf_op jit(solution)/shard_map/ppermute | solution.py:118
  435.3 33.9 %collective-permute-start.78 = (bf16[2,2,2,32,1024]{4,3,2,1,0:T(8,128)(2,1)}, bf16[2,2,2,32,1024]{4,3,2,1,0:T(8,128)(2,1)}, u32[]{:S(2)}, u32[]{:S(2)}) collective-permute-start(bf16[2,2,2,32,1024]{4,3,2,1,0:T(8,128)(2,1)} %fusion.78), channel_id=1, source_target_pairs={{0,2},{1,3},{2,0},{3,1},{4,6},{5,7},{6,4},{7,5},{8,10},{9,11},{10,... | collective-permute-start | bytes 1572872 | tf_op jit(solution)/shard_map/ppermute | solution.py:118
  440.7 34.8 %collective-permute-start.44 = (bf16[256,1024]{1,0:T(8,128)(2,1)}, bf16[256,1024]{1,0:T(8,128)(2,1)}, u32[]{:S(2)}, u32[]{:S(2)}) collective-permute-start(bf16[256,1024]{1,0:T(8,128)(2,1)} %fusion.82), channel_id=1, source_target_pairs={{0,4},{1,5},{2,6},{3,7},{4,0},{5,1},{6,2},{7,3},{8,12},{9,13},{10,... | collective-permute-start | bytes 1572872 | tf_op jit(solution)/shard_map/ppermute | solution.py:118
  460.2 39.6 %collective-permute-start.69 = (bf16[2,160,1024]{2,1,0:T(8,128)(2,1)}, bf16[2,160,1024]{2,1,0:T(8,128)(2,1)}, u32[]{:S(2)}, u32[]{:S(2)}) collective-permute-start(bf16[2,160,1024]{2,1,0:T(8,128)(2,1)} %fusion.76), channel_id=1, source_target_pairs={{0,16},{1,17},{2,18},{3,19},{4,20},{5,21},{6,22},{7,23},{8,24},{9,... | collective-permute-start | bytes 1966088 | tf_op jit(solution)/shard_map/ppermute | solution.py:118
  498.7 17.1 %collective-permute-start.81 = (bf16[2,32,1024]{2,1,0:T(8,128)(2,1)S(1)}, bf16[2,32,1024]{2,1,0:T(8,128)(2,1)S(1)}, u32[]{:S(2)}, u32[]{:S(2)}) collective-permute-start(bf16[2,32,1024]{2,1,0:T(8,128)(2,1)S(1)} %select_bitcast_fusion.38), channel_id=1, source_target_pairs={{0,1},{1,0},{2,3},{3,2},{4,5},{5,4},{6,7},{7,6},{8,9},{9,8},{10,11... | collective-permute-start | bytes 393224 | tf_op jit(solution)/shard_map/ppermute | solution.py:118
  510.6 24.3 %collective-permute-start.46 = (bf16[2,256,1024]{2,1,0:T(8,128)(2,1)}, bf16[2,256,1024]{2,1,0:T(8,128)(2,1)}, u32[]{:S(2)}, u32[]{:S(2)}) collective-permute-start(bf16[2,256,1024]{2,1,0:T(8,128)(2,1)} %pad_maximum_fusion.17), channel_id=1, source_target_pairs={{0,1},{1,0},{2,3},{3,2},{4,5},{5,4},{6,7},{7,6},{8,9},{9,8},{10,11... | collective-permute-start | bytes 3145736 | tf_op jit(solution)/shard_map/ppermute | solution.py:118
  531.9 168.0 %collective-permute-start.71 = (bf16[32,1024]{1,0:T(8,128)(2,1)}, bf16[32,1024]{1,0:T(8,128)(2,1)}, u32[]{:S(2)}, u32[]{:S(2)}) collective-permute-start(bf16[32,1024]{1,0:T(8,128)(2,1)} %slice.1377), channel_id=1, source_target_pairs={{0,0},{1,16},{2,2},{3,18},{4,4},{5,20},{6,6},{7,22},{8,8},{9,24},{... | collective-permute-start | bytes 196616 | tf_op jit(solution)/shard_map/ppermute | solution.py:342
  562.9 19.6 %collective-permute-start.54 = (bf16[512,768]{1,0:T(8,128)(2,1)S(1)}, bf16[512,768]{1,0:T(8,128)(2,1)S(1)}, u32[]{:S(2)}, u32[]{:S(2)}) collective-permute-start(bf16[512,768]{1,0:T(8,128)(2,1)S(1)} %convolution_convert_fusion.5), channel_id=1, source_target_pairs={{0,16},{1,17},{2,18},{3,19},{4,20},{5,21},{6,22},{7,23},{8,24},{9,... | collective-permute-start | bytes 2359304 | tf_op jit(solution)/shard_map/ppermute | solution.py:118
  570.5 34.5 %collective-permute-start.72 = (bf16[512,1024]{1,0:T(8,128)(2,1)S(1)}, bf16[512,1024]{1,0:T(8,128)(2,1)S(1)}, u32[]{:S(2)}, u32[]{:S(2)}) collective-permute-start(bf16[512,1024]{1,0:T(8,128)(2,1)S(1)} %convolution_convert_fusion.1), channel_id=1, source_target_pairs={{0,16},{1,17},{2,18},{3,19},{4,20},{5,21},{6,22},{7,23},{8,24},{9,... | collective-permute-start | bytes 3145736 | tf_op jit(solution)/shard_map/ppermute | solution.py:118
  570.8 41.7 %collective-permute-start.64 = (bf16[2,2,160,1024]{3,2,1,0:T(8,128)(2,1)S(1)}, bf16[2,2,160,1024]{3,2,1,0:T(8,128)(2,1)S(1)}, u32[]{:S(2)}, u32[]{:S(2)}) collective-permute-start(bf16[2,2,160,1024]{3,2,1,0:T(8,128)(2,1)S(1)} %pad_maximum_fusion.10), channel_id=1, source_target_pairs={{0,2},{1,3},{2,0},{3,1},{4,6},{5,7},{6,4},{7,5},{8,10},{9,11},{10,... | collective-permute-start | bytes 3932168 | tf_op jit(solution)/shard_map/ppermute | solution.py:118
  571.5 35.6 %collective-permute-start.47 = (bf16[2,256,1024]{2,1,0:T(8,128)(2,1)S(1)}, bf16[2,256,1024]{2,1,0:T(8,128)(2,1)S(1)}, u32[]{:S(2)}, u32[]{:S(2)}) collective-permute-start(bf16[2,256,1024]{2,1,0:T(8,128)(2,1)S(1)} %bitcast.911), channel_id=1, source_target_pairs={{0,1},{1,0},{2,3},{3,2},{4,5},{5,4},{6,7},{7,6},{8,9},{9,8},{10,11... | collective-permute-start | bytes 3145736 | tf_op jit(solution)/shard_map/ppermute | solution.py:118
  583.6 27.1 %collective-permute-start.55 = (bf16[2,2,2,32,768]{4,3,2,1,0:T(8,128)(2,1)S(1)}, bf16[2,2,2,32,768]{4,3,2,1,0:T(8,128)(2,1)S(1)}, u32[]{:S(2)}, u32[]{:S(2)}) collective-permute-start(bf16[2,2,2,32,768]{4,3,2,1,0:T(8,128)(2,1)S(1)} %fusion.88), channel_id=1, source_target_pairs={{0,2},{1,3},{2,0},{3,1},{4,6},{5,7},{6,4},{7,5},{8,10},{9,11},{10,... | collective-permute-start | bytes 1179656 | tf_op jit(solution)/shard_map/ppermute | solution.py:118
  606.4 27.5 %collective-permute-start.73 = (bf16[2,2,2,32,1024]{4,3,2,1,0:T(8,128)(2,1)S(1)}, bf16[2,2,2,32,1024]{4,3,2,1,0:T(8,128)(2,1)S(1)}, u32[]{:S(2)}, u32[]{:S(2)}) collective-permute-start(bf16[2,2,2,32,1024]{4,3,2,1,0:T(8,128)(2,1)S(1)} %fusion.77), channel_id=1, source_target_pairs={{0,2},{1,3},{2,0},{3,1},{4,6},{5,7},{6,4},{7,5},{8,10},{9,11},{10,... | collective-permute-start | bytes 1572872 | tf_op jit(solution)/shard_map/ppermute | solution.py:118
  608.5 30.5 %collective-permute-start.48 = (bf16[256,1024]{1,0:T(8,128)(2,1)}, bf16[256,1024]{1,0:T(8,128)(2,1)}, u32[]{:S(2)}, u32[]{:S(2)}) collective-permute-start(bf16[256,1024]{1,0:T(8,128)(2,1)} %fusion.83), channel_id=1, source_target_pairs={{0,4},{1,5},{2,6},{3,7},{4,0},{5,1},{6,2},{7,3},{8,12},{9,13},{10,... | collective-permute-start | bytes 1572872 | tf_op jit(solution)/shard_map/ppermute | solution.py:118
  628.3 50.4 %collective-permute-start.65 = (bf16[2,160,1024]{2,1,0:T(8,128)(2,1)}, bf16[2,160,1024]{2,1,0:T(8,128)(2,1)}, u32[]{:S(2)}, u32[]{:S(2)}) collective-permute-start(bf16[2,160,1024]{2,1,0:T(8,128)(2,1)} %fusion.75), channel_id=1, source_target_pairs={{0,16},{1,17},{2,18},{3,19},{4,20},{5,21},{6,22},{7,23},{8,24},{9,... | collective-permute-start | bytes 1966088 | tf_op jit(solution)/shard_map/ppermute | solution.py:118
  635.8 35.5 %collective-permute-start.74 = (bf16[2,2,32,1024]{3,2,1,0:T(8,128)(2,1)}, bf16[2,2,32,1024]{3,2,1,0:T(8,128)(2,1)}, u32[]{:S(2)}, u32[]{:S(2)}) collective-permute-start(bf16[2,2,32,1024]{3,2,1,0:T(8,128)(2,1)} %fusion.100), channel_id=1, source_target_pairs={{0,8},{1,9},{2,10},{3,11},{4,12},{5,13},{6,14},{7,15},{8,0},{9,1},... | collective-permute-start | bytes 786440 | tf_op jit(solution)/shard_map/ppermute | solution.py:118
  681.3 16.7 %collective-permute-start.66 = (bf16[160,1024]{1,0:T(8,128)(2,1)S(1)}, bf16[160,1024]{1,0:T(8,128)(2,1)S(1)}, u32[]{:S(2)}, u32[]{:S(2)}) collective-permute-start(bf16[160,1024]{1,0:T(8,128)(2,1)S(1)} %fusion.96), channel_id=1, source_target_pairs={{0,8},{1,9},{2,10},{3,11},{4,12},{5,13},{6,14},{7,15},{8,0},{9,1},... | collective-permute-start | bytes 983048 | tf_op jit(solution)/shard_map/ppermute | solution.py:118
  (156 other events, 1167.2 us)
